TPU v7x, 512 devices: a whole 4x8x8 slice. The times are simulated.
512 devices in a mesh: ctx: 16 (over y, core), exp: 32 (over z, x).
Axes of the slice: x: 4, y: 8, z: 8, core: 2. Of those that a mesh axis runs over, the one named last changes fastest.
Arguments:
- queries: bfloat16 [4096, 8192], P('exp', 'ctx'), may hold values from -180 to 180
- key_proj: bfloat16 [4096, 512], P('exp'), may hold values from -7 to 7
- value_matrix_rows: bfloat16 [4096, 512], P('exp'), may hold values from -6 to 6
- attn_grad: bfloat16 [4096, 8192], P('exp', 'ctx'), may hold values from -6 to 6
- moe_input: bfloat16 [4096, 4096], P('exp', 'ctx'), may hold values from -6 to 6
- moe_grad: bfloat16 [4096, 4096], P('exp', 'ctx'), may hold values from -6 to 6
- expert_ids: int32 [4096, 2], P('exp'), may hold values from 0 to 63, as said below
- route_weights: float32 [4096, 2], P('exp'), may hold values from 0.1 to 1
- gate_proj: bfloat16 [64, 4096, 768], P('exp', 'ctx'), may hold values from -0.09375 to 0.09375
- up_proj: bfloat16 [64, 4096, 768], P('exp', 'ctx'), may hold values from -0.09375 to 0.09375
- down_proj: bfloat16 [64, 768, 4096], P('exp', None, 'ctx'), may hold values from -0.21875 to 0.21875
Outputs:
- attn_out: bfloat16 [4096, 8192], P('exp', 'ctx')
- query_grad: bfloat16 [4096, 8192], P('exp', 'ctx')
- key_grad: bfloat16 [4096, 512], P('exp')
- value_grad: bfloat16 [4096, 512], P('exp')
- moe_out: bfloat16 [4096, 4096], P('exp', 'ctx')
- input_grad: bfloat16 [4096, 4096], P('exp', 'ctx')
Inputs may be any that keep to these rules, and one draw needn't show every extreme that they name: `expert_ids`: each row names 2 different experts. In each aligned block of 128 rows no expert is named more than 6 times, and one expert, the same in every block, is named exactly 6 times in every block.
All inputs are finite; a program needn't handle non-finite values.
Results may differ from a plain program's by a relative error of at most 0.019.
Values may be sent and summed in bfloat16 or wider, within the bound.
A program may use at most 64 MiB of HBM per device.

v0:
```python
import jax
import jax.numpy as jnp
from jax import lax
from jax.sharding import PartitionSpec as P

HEAD_SIZE = 128


def gate_backward(hidden_grad, gate_full, up_full):
    sigmoid_gate = jax.nn.sigmoid(gate_full)
    activated = gate_full * sigmoid_gate
    gate_back = (
        hidden_grad * up_full * sigmoid_gate * (1.0 + gate_full * (1.0 - sigmoid_gate))
    ).astype(jnp.bfloat16)
    up_back = (hidden_grad * activated).astype(jnp.bfloat16)
    return (gate_back, up_back)


def activate(gate_full, up_full):
    return (jax.nn.silu(gate_full) * up_full).astype(jnp.bfloat16)


def body(
    queries,
    key_proj,
    value_matrix_rows,
    attn_grad,
    moe_input,
    moe_grad,
    expert_ids,
    route_weights,
    gate_proj,
    up_proj,
    down_proj,
):
    ctx_count = lax.axis_size("ctx")
    exp_count = lax.axis_size("exp")
    ctx_index = lax.axis_index("ctx")
    exp_index = lax.axis_index("exp")
    tok_count = queries.shape[0]
    head_dim = HEAD_SIZE
    heads_here = queries.shape[1] // head_dim
    kv_heads = key_proj.shape[1] // head_dim
    sharers = ctx_count // kv_heads
    kv_head = ctx_index // sharers
    seq_count = tok_count * exp_count
    score_scale = head_dim ** (-0.5)
    key_pick = lax.dynamic_slice_in_dim(key_proj, kv_head * head_dim, head_dim, 1)
    value_pick = lax.dynamic_slice_in_dim(value_matrix_rows, kv_head * head_dim, head_dim, 1)
    every_key, every_value = (
        lax.all_gather(key_pick, "exp", axis=0, tiled=True),
        lax.all_gather(value_pick, "exp", axis=0, tiled=True),
    )
    query_pos = exp_index * tok_count + jnp.arange(tok_count, dtype=jnp.int32)
    key_pos = jnp.arange(seq_count, dtype=jnp.int32)
    query_heads = queries.reshape(tok_count, heads_here, head_dim)
    cotan_heads = attn_grad.reshape(tok_count, heads_here, head_dim)
    scores = (
        jnp.einsum("rhd,kd->hrk", query_heads, every_key, preferred_element_type=jnp.float32)
        * score_scale
    )
    allowed = key_pos[None, :] <= query_pos[:, None]
    scores = jnp.where(allowed[None, :, :], scores, -jnp.inf)
    log_total = jax.nn.logsumexp(scores, axis=2, keepdims=True)
    attn_probs = jnp.exp(scores - log_total).astype(jnp.bfloat16)
    attended = jnp.einsum(
        "hrk,kd->rhd", attn_probs, every_value, preferred_element_type=jnp.float32
    ).astype(jnp.bfloat16)
    row_dot = jnp.sum(cotan_heads.astype(jnp.float32) * attended.astype(jnp.float32), axis=2)
    prob_grad = jnp.einsum(
        "rhd,kd->hrk", cotan_heads, every_value, preferred_element_type=jnp.float32
    )
    score_grad = (
        attn_probs.astype(jnp.float32) * (prob_grad - jnp.transpose(row_dot)[:, :, None])
    ).astype(jnp.bfloat16)
    query_back = (
        jnp.einsum("hrk,kd->rhd", score_grad, every_key, preferred_element_type=jnp.float32)
        * score_scale
    ).astype(jnp.bfloat16)
    key_term = (
        jnp.einsum("hrk,rhd->kd", score_grad, query_heads, preferred_element_type=jnp.float32)
        * score_scale
    )
    value_term = jnp.einsum(
        "hrk,rhd->kd", attn_probs, cotan_heads, preferred_element_type=jnp.float32
    )
    kv_term = jnp.concatenate([key_term, value_term], axis=1).reshape(
        exp_count, tok_count, 2 * head_dim
    )
    kv_pieces = lax.all_to_all(
        kv_term.astype(jnp.bfloat16), "exp", split_axis=0, concat_axis=0, tiled=True
    ).astype(kv_term.dtype)
    kv_summed = jnp.sum(kv_pieces, axis=0)
    kv_every = lax.all_gather(kv_summed.astype(jnp.bfloat16), "ctx", axis=1, tiled=True).astype(
        kv_summed.dtype
    )
    kv_every = kv_every.reshape(tok_count, kv_heads, sharers, 2, head_dim).sum(axis=2)
    key_grad = kv_every[:, :, 0, :].reshape(tok_count, kv_heads * head_dim).astype(jnp.bfloat16)
    value_grad = kv_every[:, :, 1, :].reshape(tok_count, kv_heads * head_dim).astype(jnp.bfloat16)
    width_here = moe_input.shape[1]
    local_experts = gate_proj.shape[0]
    top_count = expert_ids.shape[1]
    expert_total = local_experts * exp_count
    slot_count = 2 * ((tok_count + expert_total - 2) // (expert_total - 1))
    flat_ids = expert_ids.reshape(-1)
    flat_gain = route_weights.reshape(-1)
    targets = jnp.arange(expert_total, dtype=jnp.int32)
    chosen = flat_ids[None, :] == targets[:, None]

    def first_places(flags):
        return jnp.nonzero(flags, size=slot_count, fill_value=0)[0]

    places = jax.vmap(first_places)(chosen)
    filled = jnp.arange(slot_count)[None, :] < jnp.sum(chosen, axis=1)[:, None]
    slot_token = (places // top_count).astype(jnp.int32)
    picked_gain = flat_gain[places]
    slot_gain = jnp.where(filled, picked_gain, jnp.zeros_like(picked_gain))
    send_rows = moe_input[slot_token].reshape(exp_count, local_experts, slot_count, width_here)
    send_scaled = (moe_grad[slot_token].astype(jnp.float32) * slot_gain[:, :, None]).astype(
        jnp.bfloat16
    )
    send_scaled = send_scaled.reshape(exp_count, local_experts, slot_count, width_here)
    recv_rows, recv_scaled = (
        lax.all_to_all(send_rows, "exp", split_axis=0, concat_axis=0, tiled=True),
        lax.all_to_all(send_scaled, "exp", split_axis=0, concat_axis=0, tiled=True),
    )
    gate_part = jnp.einsum(
        "sacd,adf->sacf", recv_rows, gate_proj, preferred_element_type=jnp.float32
    )
    up_part = jnp.einsum("sacd,adf->sacf", recv_rows, up_proj, preferred_element_type=jnp.float32)
    hidden_part = jnp.einsum(
        "sacd,afd->sacf", recv_scaled, down_proj, preferred_element_type=jnp.float32
    )
    gate_full, up_full = lax.psum((gate_part, up_part), "ctx")
    hidden = activate(gate_full, up_full)
    hidden_grad = lax.psum(hidden_part, "ctx")
    gate_back, up_back = gate_backward(hidden_grad, gate_full, up_full)
    route_out = jnp.einsum(
        "sacf,afd->sacd", hidden, down_proj, preferred_element_type=jnp.float32
    ).astype(jnp.bfloat16)
    route_in = (
        jnp.einsum("sacf,adf->sacd", gate_back, gate_proj, preferred_element_type=jnp.float32)
        + jnp.einsum("sacf,adf->sacd", up_back, up_proj, preferred_element_type=jnp.float32)
    ).astype(jnp.bfloat16)
    back_out, back_in = (
        lax.all_to_all(route_out, "exp", split_axis=0, concat_axis=0, tiled=True),
        lax.all_to_all(route_in, "exp", split_axis=0, concat_axis=0, tiled=True),
    )
    slot_flat = slot_token.reshape(-1)
    member = (
        slot_flat[:, None] == jnp.arange(tok_count, dtype=jnp.int32)[None, :]
    ) & filled.reshape(-1)[:, None]
    weight_table = jnp.where(member, slot_gain.reshape(-1)[:, None], 0.0)
    moe_out = jnp.einsum(
        "pt,pd->td",
        weight_table,
        back_out.reshape(-1, width_here).astype(jnp.float32),
        precision=lax.Precision.HIGHEST,
        preferred_element_type=jnp.float32,
    ).astype(jnp.bfloat16)
    input_grad = jnp.einsum(
        "pt,pd->td",
        member.astype(jnp.bfloat16),
        back_in.reshape(-1, width_here),
        preferred_element_type=jnp.float32,
    ).astype(jnp.bfloat16)
    attn_out = attended.reshape(tok_count, heads_here * head_dim)
    query_grad = query_back.reshape(tok_count, heads_here * head_dim)
    return (attn_out, query_grad, key_grad, value_grad, moe_out, input_grad)


def solution(mesh):
    placed = (
        P("exp", "ctx"),
        P("exp", None),
        P("exp", None),
        P("exp", "ctx"),
        P("exp", "ctx"),
        P("exp", "ctx"),
        P("exp", None),
        P("exp", None),
        P("exp", "ctx", None),
        P("exp", "ctx", None),
        P("exp", None, "ctx"),
    )
    return jax.shard_map(
        body,
        mesh=mesh,
        in_specs=placed,
        out_specs=(
            P("exp", "ctx"),
            P("exp", "ctx"),
            P("exp", None),
            P("exp", None),
            P("exp", "ctx"),
            P("exp", "ctx"),
        ),
        check_vma=False,
    )
```

profile of v0, /device:TPU:1, one launch (start us, length us, event | category | flops | bytes accessed | tf_op | source)
XLA Modules:
  0.0 449.1 jit_solution(22653749331773646)
XLA Ops:
  8.1 1.4 constant_dynamic-slice_fusion
  13.3 110.5 %scatter_custom_fusion = s32[384]{0:T(512)S(1)} fusion(s32[16384]{0:T(1024)S(1)} %bitcast.119, s32[16384]{0:T(1024)S(1)} %broadcast.385, s32[]{:T(128)} %constant.86.clone.1), kind=kCustom, calls=%fused_computation.107 | custom fusion | flops 16384 | bytes 1540
  125.4 2.8 gather_fusion
  128.6 2.1 gather_fusion.2
  131.8 14.0 %all-to-all-start.3 = ((bf16[32,2,6,256]{3,1,2,0:T(2,128)(2,1)}), bf16[32,2,6,256]{3,1,2,0:T(2,128)(2,1)S(1)}, u32[]{:S(2)}, u32[]{:S(2)}) async-start(bf16[32,2,6,256]{3,1,2,0:T(2,128)(2,1)} %copy.163), calls=%async_computation.3 | async-start | bytes 393216 | tf_op jit(solution)/shard_map/all_to_all | solution.py:125
  147.6 2.1 gather_fusion.1
  151.2 2.5 fusion.52
  154.8 3.0 exponential_convert_fusion
  157.9 66.6 %all-gather.4.cloned.1.call-done = bf16[4096,128]{0,1:T(8,128)(2,1)} async-done(((bf16[128,128]{0,1:T(8,128)(2,1)}), bf16[4096,128]{0,1:T(8,128)(2,1)}) %all-gather.4.cloned.1.call-update) | async-done | bytes 1048592 | tf_op jit(solution)/shard_map/all_gather | solution.py:52
  224.5 3.4 multiply_reduce_fusion
  228.5 3.3 fusion.1
  231.8 1.5 fusion.4
  233.3 6.5 %all-to-all-start.1 = ((bf16[32,2,6,256]{3,1,2,0:T(2,128)(2,1)}), bf16[32,2,6,256]{3,1,2,0:T(2,128)(2,1)S(1)}, u32[]{:S(2)}, u32[]{:S(2)}) async-start(bf16[32,2,6,256]{3,1,2,0:T(2,128)(2,1)} %copy.158), calls=%async_computation.1 | async-start | bytes 393216 | tf_op jit(solution)/shard_map/all_to_all | solution.py:124
  239.8 3.7 fusion.3
  243.5 1.9 copy_bitcast_fusion
  245.4 4.3 all-to-all-done.1
  249.7 4.9 %all-to-all-start = ((bf16[32,128,256]{1,2,0:T(8,128)(2,1)}), bf16[32,128,256]{1,2,0:T(8,128)(2,1)S(1)}, u32[]{:S(2)}, u32[]{:S(2)}) async-start(bf16[32,128,256]{1,2,0:T(8,128)(2,1)} %copy_bitcast_fusion), calls=%async_computation | async-start | bytes 4194304 | tf_op jit(solution)/shard_map/all_to_all | solution.py:90
  254.7 2.6 convolution_bitcast_fusion.3
  257.3 1.3 convolution_bitcast_fusion.4
  258.6 1.5 convolution_bitcast_fusion.2
  260.7 131.2 %all-reduce.3.cloned.1.call-done = (f32[32,2,6,768]{3,0,2,1:T(8,128)}, f32[32,2,6,768]{3,0,2,1:T(8,128)}, f32[32,2,6,768]{3,0,2,1:T(8,128)}) async-done(((f32[32,2,6,768]{3,0,2,1:T(8,128)}, f32[32,2,6,768]{3,0,2,1:T(8,128)}, f32[32,2,6,768]{3,0,2,1:T(8,128)}), (f32[32,2,6,768]{3,0,2,1:T(8,128)}, f32[32,2,6,768]{3,0,2,1:T(8,128)}, f32[32,2,6,768]{3,0,2,1:T(8,128)})) %all-reduce.3.cloned.1.call-update) | async-done | bytes 3538960 | tf_op jit(solution)/shard_map/psum | solution.py:134
  391.9 3.4 fusion.16
  396.2 2.5 fusion.9
  399.6 9.9 %all-to-all-start.4 = ((bf16[32,2,6,256]{3,1,2,0:T(2,128)(2,1)}), bf16[32,2,6,256]{3,1,2,0:T(2,128)(2,1)S(1)}, u32[]{:S(2)}, u32[]{:S(2)}) async-start(bf16[32,2,6,256]{3,1,2,0:T(2,128)(2,1)} %copy.165), calls=%async_computation.4 | async-start | bytes 393216 | tf_op jit(solution)/shard_map/all_to_all | solution.py:147
  409.9 2.2 fusion.8
  412.9 6.4 %all-to-all-done.4 = bf16[32,2,6,256]{3,1,2,0:T(2,128)(2,1)S(1)} async-done(((bf16[32,2,6,256]{3,1,2,0:T(2,128)(2,1)}), bf16[32,2,6,256]{3,1,2,0:T(2,128)(2,1)S(1)}, u32[]{:S(2)}, u32[]{:S(2)}) %all-to-all-start.4) | async-done | bytes 196640 | tf_op jit(solution)/shard_map/all_to_all | solution.py:147
  419.4 3.9 all-to-all-start.2
  423.3 3.0 fusion.7
  427.9 5.2 %all-to-all-done.2 = bf16[32,2,6,256]{3,1,2,0:T(2,128)(2,1)S(1)} async-done(((bf16[32,2,6,256]{3,1,2,0:T(2,128)(2,1)}), bf16[32,2,6,256]{3,1,2,0:T(2,128)(2,1)S(1)}, u32[]{:S(2)}, u32[]{:S(2)}) %all-to-all-start.2) | async-done | bytes 196640 | tf_op jit(solution)/shard_map/all_to_all | solution.py:146
  434.2 1.2 convolution_convert_fusion.2
  435.4 3.4 all-gather.8.cloned.1.call-done
  438.7 1.4 reduce.3
  (98 shorter events, 19.8 us)
Async XLA Ops:
  8.0 249.3 %copy-start = (bf16[2,256,768]{2,1,0:T(8,128)(2,1)S(1)}, bf16[2,256,768]{2,1,0:T(8,128)(2,1)}, u32[]{:S(2)}) copy-start(bf16[2,256,768]{2,1,0:T(8,128)(2,1)} %param.19) | copy-start | bytes 2359300
  8.0 143.2 %all-gather.6.cloned.1.call-start = ((), (), s32[]{:S(2)}) async-start(), calls=%async_computation.6 | async-start | bytes 1081344 | tf_op jit(solution)/shard_map/all_gather | solution.py:51
  125.3 3.2 copy-start.2
  128.6 19.0 %copy-start.3 = (bf16[128,256]{1,0:T(8,128)(2,1)S(1)}, bf16[128,256]{1,0:T(8,128)(2,1)}, u32[]{:S(2)}) copy-start(bf16[128,256]{1,0:T(8,128)(2,1)} %param.15) | copy-start | bytes 196612
  131.8 101.5 %all-to-all-start.3 = ((bf16[32,2,6,256]{3,1,2,0:T(2,128)(2,1)}), bf16[32,2,6,256]{3,1,2,0:T(2,128)(2,1)S(1)}, u32[]{:S(2)}, u32[]{:S(2)}) async-start(bf16[32,2,6,256]{3,1,2,0:T(2,128)(2,1)} %copy.163), calls=%async_computation.3 | async-start | bytes 393216 | tf_op jit(solution)/shard_map/all_to_all | solution.py:125
  145.8 5.1 %copy-start.8 = (bf16[128,512]{1,0:T(8,128)(2,1)S(1)}, bf16[128,512]{1,0:T(8,128)(2,1)}, u32[]{:S(2)}) copy-start(bf16[128,512]{1,0:T(8,128)(2,1)} %param.11) | copy-start | bytes 393220
  145.8 78.6 %all-gather.4.cloned.1.call-start = ((), (), s32[]{:S(2)}) async-start(), calls=%async_computation.5 | async-start | bytes 1081344 | tf_op jit(solution)/shard_map/all_gather | solution.py:52
  146.8 4.2 copy-start.9
  224.5 3.7 copy-start.1
  224.5 4.0 copy-start.4
  233.3 16.4 %all-to-all-start.1 = ((bf16[32,2,6,256]{3,1,2,0:T(2,128)(2,1)}), bf16[32,2,6,256]{3,1,2,0:T(2,128)(2,1)S(1)}, u32[]{:S(2)}, u32[]{:S(2)}) async-start(bf16[32,2,6,256]{3,1,2,0:T(2,128)(2,1)} %copy.158), calls=%async_computation.1 | async-start | bytes 393216 | tf_op jit(solution)/shard_map/all_to_all | solution.py:124
  249.7 145.5 %all-to-all-start = ((bf16[32,128,256]{1,2,0:T(8,128)(2,1)}), bf16[32,128,256]{1,2,0:T(8,128)(2,1)S(1)}, u32[]{:S(2)}, u32[]{:S(2)}) async-start(bf16[32,128,256]{1,2,0:T(8,128)(2,1)} %copy_bitcast_fusion), calls=%async_computation | async-start | bytes 4194304 | tf_op jit(solution)/shard_map/all_to_all | solution.py:90
  254.6 137.2 %all-reduce.3.cloned.1.call-start = ((), (), s32[]{:S(2)}) async-start(), calls=%async_computation.8 | async-start | bytes 7077888 | tf_op jit(solution)/shard_map/psum | solution.py:134
  254.7 3.9 copy-start.6
  260.1 178.6 %all-gather.8.cloned.1.call-start = ((), (), s32[]{:S(2)}) async-start(), calls=%async_computation.7 | async-start | bytes 1114112 | tf_op jit(solution)/shard_map/all_gather | solution.py:94
  396.2 13.7 %copy-start.7 = (bf16[2,768,256]{2,1,0:T(8,128)(2,1)S(1)}, bf16[2,768,256]{2,1,0:T(8,128)(2,1)}, u32[]{:S(2)}) copy-start(bf16[2,768,256]{2,1,0:T(8,128)(2,1)} %param.21) | copy-start | bytes 2359300
  399.6 19.8 %all-to-all-start.4 = ((bf16[32,2,6,256]{3,1,2,0:T(2,128)(2,1)}), bf16[32,2,6,256]{3,1,2,0:T(2,128)(2,1)S(1)}, u32[]{:S(2)}, u32[]{:S(2)}) async-start(bf16[32,2,6,256]{3,1,2,0:T(2,128)(2,1)} %copy.165), calls=%async_computation.4 | async-start | bytes 393216 | tf_op jit(solution)/shard_map/all_to_all | solution.py:147
  409.9 13.4 %copy-start.5 = (bf16[4096,128]{1,0:T(8,128)(2,1)S(1)}, bf16[4096,128]{1,0:T(8,128)(2,1)}, u32[]{:S(2)}) copy-start(bf16[4096,128]{1,0:T(8,128)(2,1)} %all-gather.6.cloned.1.call-done) | copy-start | bytes 3145732
  419.4 13.7 %all-to-all-start.2 = ((bf16[32,2,6,256]{3,1,2,0:T(2,128)(2,1)}), bf16[32,2,6,256]{3,1,2,0:T(2,128)(2,1)S(1)}, u32[]{:S(2)}, u32[]{:S(2)}) async-start(bf16[32,2,6,256]{3,1,2,0:T(2,128)(2,1)} %copy.161), calls=%async_computation.2 | async-start | bytes 393216 | tf_op jit(solution)/shard_map/all_to_all | solution.py:146
Sparse Core Ops, SparseCore 0:
  12.6 82.6 all-gather.5
  150.3 74.1 all-gather.3
Sparse Core Ops, SparseCore 1:
  260.2 131.6 all-reduce.2
  396.3 42.4 all-gather.7
where the time goes:
time: 451 us; the launch traced here: 449 us
  waiting for transfers between devices  217 us (48%)
  other arithmetic  122 us (27%)
  starting transfers between devices  39.8 us (9%)
  matrix products  32.8 us (7%)
  local copies, waits for them, and re-layouts  21.3 us (5%)
  between operations  16 us (4%)
    psum x1, waiting for transfers between devices, body(): gate_full, up_full = lax.psum((gate_part, up_part), 'ctx')  131 us
    unnamed x4, other arithmetic  112 us
    all_gather x1, waiting for transfers between devices, body(): lax.all_gather(value_pick, 'exp', axis=0, tiled=True)  66.6 us
    all_to_all x1, starting transfers between devices, body(): lax.all_to_all(send_scaled, 'exp', split_axis=0, concat_axis=0, tiled=True)  14 us
    all_to_all x1, starting transfers between devices, body(): lax.all_to_all(route_in, 'exp', split_axis=0, concat_axis=0, tiled=True)  9.9 us
  transfers between devices with their start and end apart: 9, of which 6 were waited for; matrix products, arithmetic and copies ran while one was open for 38% of the time, Pallas kernels for 0%

commit v1 on v0

v1 whole, which is shorter than its diff:
```python
import functools

import jax
import jax.numpy as jnp
from jax import lax
from jax.experimental import pallas as pl
from jax.experimental.pallas import tpu as pltpu
from jax.sharding import PartitionSpec as P

MESH = pl.DeviceIdType.MESH
F32 = jnp.float32
BF16 = jnp.bfloat16
HEAD = 128
NX, NZ, NY = 4, 8, 8
NE = NX * NZ
TOK = 128
LOCAL = 2
EXPERTS = LOCAL * NE
SLOT = 6
GROUP = LOCAL * SLOT
SLAB = 4 * GROUP
ROWS = NE * GROUP
FF = 768
HALF = FF // 2
YROWS = ROWS // NY
SCALE = HEAD ** (-0.5)
VMEM_LIMIT = 60 * 1024 * 1024


def dot(a, b):
    return jnp.dot(a, b, preferred_element_type=F32)


def dot_t(a, b):
    return lax.dot_general(a, b, (((1,), (1,)), ((), ())), preferred_element_type=F32)


def t_dot(a, b):
    return lax.dot_general(a, b, (((0,), (0,)), ((), ())), preferred_element_type=F32)


def fdiv(a, n):
    return jnp.floor((a + 0.5) * (1.0 / n))


def fiota(shape, dim):
    return lax.broadcasted_iota(jnp.int32, shape, dim).astype(F32)


def route_tables(ids):
    lane = lax.broadcasted_iota(jnp.int32, (TOK, EXPERTS), 1)
    first = jnp.where(ids[:, 0:1] == lane, 1.0, 0.0)
    second = jnp.where(ids[:, 1:2] == lane, 1.0, 0.0)
    row = lax.broadcasted_iota(jnp.int32, (TOK, TOK), 0)
    col = lax.broadcasted_iota(jnp.int32, (TOK, TOK), 1)
    before = jnp.where(col < row, 1.0, 0.0).astype(BF16)
    place = dot(before, (first + second).astype(BF16)) + 1.0
    return (first * place).astype(BF16), (second * place).astype(BF16)


def slab_index(p):
    dest = fdiv(p, SLAB)
    inner = p - dest * SLAB
    quarter = fdiv(inner, GROUP)
    inner = inner - quarter * GROUP
    local = fdiv(inner, SLOT)
    slot = inner - local * SLOT
    return dest * LOCAL + local, quarter, slot


def prep_kernel(ids_ref, gain_ref, x_ref, g_ref, out_ref):
    v0, v1 = route_tables(ids_ref[...])
    total = NE * SLAB
    expert, quarter, slot = slab_index(fiota((total, 1), 0))
    pick = jnp.where(expert == fiota((total, EXPERTS), 1), 1.0, 0.0).astype(BF16)
    y0 = dot_t(pick, v0)
    y1 = dot_t(pick, v1)
    want = slot + 1.0
    hit0 = jnp.where(y0 == want, 1.0, 0.0)
    hit1 = jnp.where(y1 == want, 1.0, 0.0)
    both = hit0 + hit1
    q = [jnp.where(quarter == float(i), 1.0, 0.0) for i in range(4)]
    table = jnp.concatenate(
        [both * q[0], both * q[1], hit0 * q[2], hit0 * q[3], hit1 * q[2], hit1 * q[3]], axis=1
    ).astype(BF16)
    x = x_ref[...]
    g = g_ref[...].astype(F32)
    gain = gain_ref[...]
    s0 = (g * gain[:, 0:1]).astype(BF16)
    s1 = (g * gain[:, 1:2]).astype(BF16)
    rows = jnp.concatenate(
        [x[:, :128], x[:, 128:], s0[:, :128], s0[:, 128:], s1[:, :128], s1[:, 128:]], axis=0
    )
    out_ref[...] = dot(table, rows).astype(BF16)


def combine_kernel(ids_ref, gain_ref, back_ref, kvg_ref, out_ref, in_ref, kg_ref, vg_ref):
    v0, v1 = route_tables(ids_ref[...])
    total = NE * SLAB
    expert, quarter, slot = slab_index(fiota((1, total), 1))
    pick = jnp.where(expert == fiota((EXPERTS, total), 0), 1.0, 0.0).astype(BF16)
    y0 = dot(v0, pick)
    y1 = dot(v1, pick)
    want = slot + 1.0
    hit0 = jnp.where(y0 == want, 1.0, 0.0)
    hit1 = jnp.where(y1 == want, 1.0, 0.0)
    both = hit0 + hit1
    q = [jnp.where(quarter == float(i), 1.0, 0.0) for i in range(4)]
    back = back_ref[...]
    gain = gain_ref[...]
    for i in range(2):
        part0 = dot((hit0 * q[i]).astype(BF16), back)
        part1 = dot((hit1 * q[i]).astype(BF16), back)
        out_ref[:, i * 128 : (i + 1) * 128] = (
            part0 * gain[:, 0:1] + part1 * gain[:, 1:2]
        ).astype(BF16)
        in_ref[:, i * 128 : (i + 1) * 128] = dot((both * q[2 + i]).astype(BF16), back).astype(BF16)
    kg_ref[...] = kvg_ref[0]
    vg_ref[...] = kvg_ref[1]


PACK = 8 * GROUP


def pack_table(transposed):
    n = 4 * PACK
    shape = (n, n)
    r = fiota((1, n) if transposed else (n, 1), 1 if transposed else 0)
    quarter = fdiv(r, PACK)
    inner = r - quarter * PACK
    source = fdiv(inner, GROUP)
    p = source * SLAB + quarter * GROUP + (inner - source * GROUP)
    return jnp.where(p == fiota(shape, 0 if transposed else 1), 1.0, 0.0).astype(BF16)


def first_local(rows):
    r = fiota((rows, 1), 0)
    inner = r - fdiv(r, GROUP) * GROUP
    return inner < float(SLOT)


def moe_in_kernel(recv_ref, gate_ref, up_ref, down_ref, out_ref):
    table = pack_table(False)
    parts = [[], [], [], []]
    n = 4 * PACK
    for g in range(NE // 8):
        packed = dot(table, recv_ref[g * n : (g + 1) * n, :]).astype(BF16)
        for i in range(4):
            parts[i].append(packed[i * PACK : (i + 1) * PACK, :])
    cols = [jnp.concatenate(p, axis=0) for p in parts]
    rows = jnp.concatenate(cols[:2], axis=1)
    scaled = jnp.concatenate(cols[2:], axis=1)
    first = first_local(ROWS)
    for m in range(3):
        if m < 2:
            w_ref = gate_ref if m == 0 else up_ref
            full = jnp.where(first, dot(rows, w_ref[0]), dot(rows, w_ref[1]))
        else:
            full = jnp.where(first, dot_t(scaled, down_ref[0]), dot_t(scaled, down_ref[1]))
        full = full.astype(BF16)
        for k in range(2):
            for y in range(NY):
                out_ref[k, y, m] = full[y * YROWS : (y + 1) * YROWS, k * HALF : (k + 1) * HALF]


def moe_out_kernel(full_ref, gate_ref, up_ref, down_ref, out_ref):
    first = first_local(ROWS)

    def both(m, weight, transposed):
        halves = [full_ref[k, :, m].reshape(ROWS, HALF) for k in range(2)]
        whole = jnp.concatenate(halves, axis=1)
        f = dot_t if transposed else dot
        return jnp.where(first, f(whole, weight[0]), f(whole, weight[1]))

    route_out = both(0, down_ref, False).astype(BF16)
    route_in = (both(1, gate_ref, True) + both(2, up_ref, True)).astype(BF16)
    quarters = [route_out[:, :128], route_out[:, 128:], route_in[:, :128], route_in[:, 128:]]
    table = pack_table(True)
    n = 4 * PACK
    for g in range(NE // 8):
        stack = jnp.concatenate([q[g * PACK : (g + 1) * PACK] for q in quarters], axis=0)
        out_ref[g * n : (g + 1) * n, :] = dot(table, stack).astype(BF16)


CHUNK = 512


def attn_kernel(q_ref, kv_ref, do_ref, out_ref, dq_ref, dkv_ref, s_ref, e_ref):
    heads = q_ref.shape[1] // HEAD
    width = heads * TOK
    per = CHUNK // (NX * TOK)
    chunks = NZ // per
    base = lax.axis_index("exp") * TOK
    q = jnp.concatenate([q_ref[:, h * HEAD : (h + 1) * HEAD] for h in range(heads)], axis=0)
    do = jnp.concatenate([do_ref[:, h * HEAD : (h + 1) * HEAD] for h in range(heads)], axis=0)
    lane = lax.broadcasted_iota(jnp.int32, (1, width), 1)
    q_pos = base + jnp.bitwise_and(lane, TOK - 1)
    row = lax.broadcasted_iota(jnp.int32, (CHUNK, 1), 0)

    def load(which, j):
        return kv_ref[which, pl.ds(j * per, per)].reshape(CHUNK, HEAD)

    def scores(j, m):
        s = dot_t(load(0, j), q) * SCALE
        s = jnp.where(row + j * CHUNK <= q_pos, s, -jnp.inf)
        s_ref[j] = s
        return jnp.maximum(m, jnp.max(s, axis=0, keepdims=True))

    m = lax.fori_loop(0, chunks, scores, jnp.full((1, width), -jnp.inf, F32))

    def values(j, carry):
        l, o = carry
        e = jnp.exp(s_ref[j] - m)
        e16 = e.astype(BF16)
        e_ref[j] = e16
        return l + jnp.sum(e, axis=0, keepdims=True), o + t_dot(load(1, j), e16)

    l, o = lax.fori_loop(
        0, chunks, values, (jnp.zeros((1, width), F32), jnp.zeros((HEAD, width), F32))
    )
    inv = 1.0 / l
    o16 = (o * inv).astype(BF16)
    o_r = o16.astype(F32).T
    delta_parts = []
    for h in range(heads):
        piece = o_r[h * TOK : (h + 1) * TOK, :]
        out_ref[:, h * HEAD : (h + 1) * HEAD] = piece.astype(BF16)
    do_t = do.astype(F32).T
    delta = jnp.sum(do_t * o16.astype(F32), axis=0, keepdims=True)

    def back(j, dq):
        k = load(0, j)
        dp = dot_t(load(1, j), do)
        p = e_ref[j].astype(F32) * inv
        ds = (p * (dp - delta)).astype(BF16)
        p16 = p.astype(BF16)
        dk = (dot(ds, q) * SCALE).astype(BF16)
        dv = dot(p16, do).astype(BF16)
        dkv_ref[0, pl.ds(j * per, per)] = dk.reshape(per, NX, TOK, HEAD)
        dkv_ref[1, pl.ds(j * per, per)] = dv.reshape(per, NX, TOK, HEAD)
        return dq + t_dot(k, ds)

    dq = lax.fori_loop(0, chunks, back, jnp.zeros((HEAD, width), F32))
    dq_r = (dq * SCALE).T
    for h in range(heads):
        dq_ref[:, h * HEAD : (h + 1) * HEAD] = dq_r[h * TOK : (h + 1) * TOK, :].astype(BF16)


class Place:
    def __init__(self):
        self.e = lax.axis_index("exp")
        self.c = lax.axis_index("ctx")
        self.z, self.x = self.e // NX, self.e % NX
        self.y, self.k = self.c // 2, self.c % 2
        self.sgn = 1 - 2 * self.k
        self.mate = {"exp": self.e, "ctx": self.y * 2 + 1 - self.k}
        self.twin = {"exp": self.e, "ctx": (self.y + 1 - 2 * (self.y % 2)) * 2 + self.k}

    def at_z(self, step):
        return (self.z + self.sgn * step + 2 * NZ) % NZ

    def at_x(self, step):
        return (self.x + self.sgn * step + 2 * NX) % NX

    def at_y(self, step):
        return (self.y + self.sgn * step + 2 * NY) % NY

    def dev_z(self, step):
        return {"exp": self.at_z(step) * NX + self.x, "ctx": self.c}

    def dev_x(self, step):
        return {"exp": self.z * NX + self.at_x(step), "ctx": self.c}

    def dev_y(self, step):
        return {"exp": self.e, "ctx": self.at_y(step) * 2 + self.k}


def remote(src, dst, send, recv, device):
    return pltpu.make_async_remote_copy(
        src_ref=src, dst_ref=dst, send_sem=send, recv_sem=recv, device_id=device,
        device_id_type=MESH,
    )


def greet(devices, far):
    barrier = pltpu.get_barrier_semaphore()
    for device in devices:
        pl.semaphore_signal(barrier, inc=1, device_id=device, device_id_type=MESH)
    count = len(devices)
    if far is not None:

        def one(o, carry):
            peer = (far.e + o) % NE
            pl.semaphore_signal(
                barrier, inc=1, device_id={"exp": peer, "ctx": far.c}, device_id_type=MESH
            )
            return carry

        lax.fori_loop(1, NE, one, 0)
        count += NE - 1
    pl.semaphore_wait(barrier, count)


def exchange(here, send_ref, recv_ref, send_sem, recv_sem):
    def desc(o):
        dest = (here.e + o) % NE
        return remote(
            send_ref.at[dest], recv_ref.at[here.e], send_sem.at[o], recv_sem.at[o],
            {"exp": dest, "ctx": here.c},
        )

    def incoming(o):
        source = (here.e + NE - o) % NE
        return remote(
            send_ref.at[source], recv_ref.at[source], send_sem.at[o], recv_sem.at[o],
            {"exp": source, "ctx": here.c},
        )

    def begin(first, last):
        def go(o, carry):
            desc(o).start()
            return carry

        lax.fori_loop(first, last, go, 0)

    def finish():
        def go(o, carry):
            desc(o).wait_send()
            incoming(o).wait_recv()
            return carry

        lax.fori_loop(1, NE, go, 0)

    return begin, finish


def drive(*chains):
    live = list(chains)
    while live:
        for chain in list(live):
            try:
                next(chain)
            except StopIteration:
                live.remove(chain)


def spread_kernel(
    send_ref, key_ref, val_ref, kv_ref, recv_ref, s_far, r_far, s_x, r_x, s_z, r_z, s_m, r_m, s_l
):
    here = Place()
    greet([here.mate], here)
    begin, finish = exchange(here, send_ref, recv_ref, s_far, r_far)
    k, z, x = here.k, here.z, here.x
    cols = pl.ds(pl.multiple_of((here.y // 2) * HEAD, HEAD), HEAD)
    own = kv_ref.at[k, z, x]

    @pl.when(k == 0)
    def _():
        c = pltpu.make_async_copy(key_ref.at[:, cols], own, s_l.at[0])
        c.start()
        c.wait()

    @pl.when(k == 1)
    def _():
        c = pltpu.make_async_copy(val_ref.at[:, cols], own, s_l.at[0])
        c.start()
        c.wait()

    local = pltpu.make_async_copy(send_ref.at[here.e], recv_ref.at[here.e], s_l.at[1])
    local.start()

    def block(step):
        return kv_ref.at[k, z, here.at_x(step)]

    def slab(step):
        return kv_ref.at[k, here.at_z(step)]

    def xcopy(i, origin, to):
        return remote(block(origin), block(origin), s_x.at[i], r_x.at[i], here.dev_x(to))

    sends = [xcopy(0, 0, 1), xcopy(2, 0, -1)]
    sends[0].start()
    sends[1].start()
    begin(1, 9)
    xcopy(0, -1, 1).wait_recv()
    c = xcopy(1, -1, 1)
    c.start()
    sends.append(c)
    xcopy(2, 1, -1).wait_recv()
    xcopy(1, -2, 1).wait_recv()

    def zcopy(i, origin, to):
        return remote(slab(origin), slab(origin), s_z.at[i], r_z.at[i], here.dev_z(to))

    def mcopy(i, origin):
        return remote(slab(origin), slab(origin), s_m.at[i], r_m.at[i], here.mate)

    half = NZ // 2
    a = zcopy(0, 0, 1)
    a.start()
    b = zcopy(half, 0, -1)
    b.start()
    m = mcopy(0, 0)
    m.start()
    sends += [a, b, m]
    bounds = [9, 17, 25, 32, 32]
    for s in range(1, half + 1):
        begin(bounds[s - 1], bounds[s])
        zcopy(s - 1, -s, 1).wait_recv()
        if s < half:
            c = zcopy(s, -s, 1)
            c.start()
            sends.append(c)
        m = mcopy(s, -s)
        m.start()
        sends.append(m)
        if s < half:
            zcopy(half + s - 1, s, -1).wait_recv()
            if s < half - 1:
                c = zcopy(half + s, s, -1)
                c.start()
                sends.append(c)
            m = mcopy(half + s, s)
            m.start()
            sends.append(m)
    other = 1 - k

    def from_mate(i, step):
        spot = kv_ref.at[other, here.at_z(-step)]
        return remote(spot, spot, s_m.at[i], r_m.at[i], here.mate)

    for s in range(0, half + 1):
        from_mate(s, -s).wait_recv()
        if 0 < s < half:
            from_mate(half + s, s).wait_recv()
    for c in sends:
        c.wait_send()
    finish()
    local.wait()


def add16(*refs):
    total = refs[0].astype(F32)
    for r in refs[1:]:
        total = total + r.astype(F32)
    return total


def reduce_kernel(
    part_ref, dkv_ref, full_ref, kg_ref,
    pmate, ysend, yrecv, dmate, zsend, zrecv, own4, xsend, xrecv, tsend, trecv,
    s_pm, r_pm, s_y, r_y, s_g, r_g, s_gm, r_gm, s_dm, r_dm, s_z, r_z, s_x, r_x, s_t, r_t,
):
    here = Place()
    k = here.k
    greet(
        [here.mate, here.twin, here.dev_z(1), here.dev_z(-1), here.dev_x(1), here.dev_x(-1),
         here.dev_y(1), here.dev_y(-1)],
        None,
    )
    half = NY // 2
    sends = []

    def go(c):
        c.start()
        sends.append(c)

    order = [4, -3, 3, -2, 2, -1, 1, 0]
    for i, step in enumerate(order):
        d = here.at_y(-step)
        go(remote(part_ref.at[1 - k, d], pmate.at[d], s_pm.at[i], r_pm.at[i], here.mate))
        d = here.at_z(-step)
        go(remote(dkv_ref.at[1 - k, d], dmate.at[d], s_dm.at[i], r_dm.at[i], here.mate))

    def part_in(i):
        d = here.at_y(order[i])
        remote(part_ref.at[k, d], pmate.at[d], s_pm.at[i], r_pm.at[i], here.mate).wait_recv()
        return d

    def dkv_in(i):
        d = here.at_z(order[i])
        remote(dkv_ref.at[k, d], dmate.at[d], s_dm.at[i], r_dm.at[i], here.mate).wait_recv()
        return d

    def yslot(i, to):
        return remote(ysend.at[i], yrecv.at[i], s_y.at[i], r_y.at[i], here.dev_y(to))

    def zslot(i, to):
        return remote(zsend.at[i], zrecv.at[i], s_z.at[i], r_z.at[i], here.dev_z(to))

    def chain_y():
        for s in range(half):
            d = part_in(order.index(half - s))
            if s == 0:
                ysend[0] = add16(part_ref[k, d], pmate[d]).astype(BF16)
            else:
                yslot(s - 1, 1).wait_recv()
                ysend[s] = add16(part_ref[k, d], pmate[d], yrecv[s - 1]).astype(BF16)
            go(yslot(s, 1))
            yield
            if s < half - 1:
                d = part_in(order.index(-(half - 1 - s)))
                if s == 0:
                    ysend[half] = add16(part_ref[k, d], pmate[d]).astype(BF16)
                else:
                    yslot(half + s - 1, -1).wait_recv()
                    ysend[half + s] = add16(
                        part_ref[k, d], pmate[d], yrecv[half + s - 1]
                    ).astype(BF16)
                go(yslot(half + s, -1))
                yield
        d = part_in(order.index(0))
        yslot(2 * half - 2, -1).wait_recv()
        yslot(half - 1, 1).wait_recv()
        total = add16(part_ref[k, d], pmate[d], yrecv[2 * half - 2], yrecv[half - 1])
        gate, up, hidden_grad = total[0], total[1], total[2]
        sig = 1.0 / (1.0 + jnp.exp(-gate))
        act = gate * sig
        full_ref[k, here.y, 0] = (act * up).astype(BF16)
        full_ref[k, here.y, 1] = (hidden_grad * up * sig * (1.0 + gate * (1.0 - sig))).astype(BF16)
        full_ref[k, here.y, 2] = (hidden_grad * act).astype(BF16)

        def gcopy(i, origin, to):
            spot = full_ref.at[k, here.at_y(origin)]
            return remote(spot, spot, s_g.at[i], r_g.at[i], here.dev_y(to))

        def mcopy(i, origin):
            spot = full_ref.at[k, here.at_y(origin)]
            return remote(spot, spot, s_gm.at[i], r_gm.at[i], here.mate)

        go(gcopy(0, 0, 1))
        go(gcopy(half, 0, -1))
        go(mcopy(0, 0))
        yield
        for s in range(1, half + 1):
            gcopy(s - 1, -s, 1).wait_recv()
            if s < half:
                go(gcopy(s, -s, 1))
            go(mcopy(s, -s))
            if s < half:
                gcopy(half + s - 1, s, -1).wait_recv()
                if s < half - 1:
                    go(gcopy(half + s, s, -1))
                go(mcopy(half + s, s))
            yield

        def from_mate(i, step):
            spot = full_ref.at[1 - k, here.at_y(step)]
            remote(spot, spot, s_gm.at[i], r_gm.at[i], here.mate).wait_recv()

        for s in range(0, half + 1):
            from_mate(s, s)
            if 0 < s < half:
                from_mate(half + s, -s)

    def chain_z():
        for s in range(half):
            d = dkv_in(order.index(half - s))
            if s == 0:
                zsend[0] = add16(dkv_ref[k, d], dmate[d]).astype(BF16)
            else:
                zslot(s - 1, 1).wait_recv()
                zsend[s] = add16(dkv_ref[k, d], dmate[d], zrecv[s - 1]).astype(BF16)
            go(zslot(s, 1))
            yield
            if s < half - 1:
                d = dkv_in(order.index(-(half - 1 - s)))
                if s == 0:
                    zsend[half] = add16(dkv_ref[k, d], dmate[d]).astype(BF16)
                else:
                    zslot(half + s - 1, -1).wait_recv()
                    zsend[half + s] = add16(
                        dkv_ref[k, d], dmate[d], zrecv[half + s - 1]
                    ).astype(BF16)
                go(zslot(half + s, -1))
                yield
        d = dkv_in(order.index(0))
        zslot(2 * half - 2, -1).wait_recv()
        zslot(half - 1, 1).wait_recv()
        own4[...] = add16(dkv_ref[k, d], dmate[d], zrecv[2 * half - 2], zrecv[half - 1])

        def xslot(i, to):
            return remote(xsend.at[i], xrecv.at[i], s_x.at[i], r_x.at[i], here.dev_x(to))

        xsend[0] = own4[here.at_x(2)].astype(BF16)
        go(xslot(0, 1))
        xsend[2] = own4[here.at_x(-1)].astype(BF16)
        go(xslot(2, -1))
        yield
        xslot(0, 1).wait_recv()
        xsend[1] = add16(own4[here.at_x(1)], xrecv[0]).astype(BF16)
        go(xslot(1, 1))
        yield
        xslot(2, -1).wait_recv()
        xslot(1, 1).wait_recv()
        tsend[...] = add16(own4[here.x], xrecv[2], xrecv[1]).astype(BF16)
        t = remote(tsend, trecv, s_t.at[0], r_t.at[0], here.twin)
        go(t)
        yield
        t.wait_recv()
        kg_ref[...] = add16(tsend[...], trecv[...]).astype(BF16)

    drive(chain_z(), chain_y())
    for c in sends:
        c.wait_send()


def return_kernel(
    send_ref, kg_ref, recv_ref, kvg_ref, s_far, r_far, s_y, r_y, s_m, r_m, s_l
):
    here = Place()
    k = here.k
    greet([here.mate] + [here.dev_y(s) for s in (2, 4, 6)], here)
    begin, finish = exchange(here, send_ref, recv_ref, s_far, r_far)

    def cols(step):
        head = here.at_y(step) // 2
        return pl.ds(pl.multiple_of(head * HEAD, HEAD), HEAD)

    def spot(which, step):
        return kvg_ref.at[which, :, cols(step)]

    sends = []

    def go(c):
        c.start()
        sends.append(c)

    for i, step in enumerate((2, 4, 6)):
        go(remote(kg_ref, spot(k, 0), s_y.at[i], r_y.at[i], here.dev_y(step)))
    go(remote(kg_ref, spot(k, 0), s_m.at[3], r_m.at[3], here.mate))
    mine = pltpu.make_async_copy(kg_ref, spot(k, 0), s_l.at[0])
    mine.start()
    local = pltpu.make_async_copy(send_ref.at[here.e], recv_ref.at[here.e], s_l.at[1])
    local.start()
    begin(1, NE)
    for i, step in enumerate((2, 4, 6)):
        remote(kg_ref, spot(k, -step), s_y.at[i], r_y.at[i], here.dev_y(-step)).wait_recv()
        go(remote(spot(k, -step), spot(k, -step), s_m.at[i], r_m.at[i], here.mate))
    for i, step in enumerate((2, 4, 6)):
        remote(
            spot(1 - k, step), spot(1 - k, step), s_m.at[i], r_m.at[i], here.mate
        ).wait_recv()
    remote(kg_ref, spot(1 - k, 0), s_m.at[3], r_m.at[3], here.mate).wait_recv()
    for c in sends:
        c.wait_send()
    finish()
    mine.wait()
    local.wait()


def vmem():
    return pl.BlockSpec(memory_space=pltpu.VMEM)


def dma(n):
    return pltpu.SemaphoreType.DMA((n,))


def call(kernel, outs, scratch, *args, specs=None, collective=None, name=None, flops=0):
    params = {"vmem_limit_bytes": VMEM_LIMIT}
    if collective is not None:
        params.update(collective_id=collective, has_side_effects=True)
    return pl.pallas_call(
        kernel,
        out_shape=outs,
        in_specs=specs or [vmem()] * len(args),
        out_specs=jax.tree.map(lambda o: vmem(), outs),
        scratch_shapes=scratch,
        compiler_params=pltpu.CompilerParams(**params),
        name=name,
    )(*args)


def shape(*dims, dtype=BF16):
    return jax.ShapeDtypeStruct(dims, dtype)


def body(q, key, val, do, x, g, ids, gain, gate, up, down):
    send = call(prep_kernel, shape(NE * SLAB, 128), [], ids, gain, x, g, name="prep")
    hbm = pl.BlockSpec(memory_space=pl.ANY)
    kv, recv = call(
        spread_kernel,
        (shape(2, NZ, NX, TOK, HEAD), shape(NE, SLAB, 128)),
        [dma(NE), dma(NE), dma(3), dma(3), dma(8), dma(8), dma(8), dma(8), dma(2)],
        send.reshape(NE, SLAB, 128), key, val,
        specs=[vmem(), hbm, hbm], collective=0, name="spread",
    )
    part = call(
        moe_in_kernel, shape(2, NY, 3, YROWS, HALF), [],
        recv.reshape(NE * SLAB, 128), gate, up, down, name="moe_in",
    )
    heads = q.shape[1] // HEAD
    steps = NE * TOK // CHUNK
    attn_out, dq, dkv = call(
        attn_kernel,
        (shape(TOK, q.shape[1]), shape(TOK, q.shape[1]), shape(2, NZ, NX, TOK, HEAD)),
        [pltpu.VMEM((steps, CHUNK, heads * TOK), F32), pltpu.VMEM((steps, CHUNK, heads * TOK), BF16)],
        q, kv, do, name="attn",
    )
    yslab = (3, YROWS, HALF)
    zslab = (NX, TOK, HEAD)
    block = (TOK, HEAD)
    full, kg = call(
        reduce_kernel,
        (shape(2, NY, *yslab), shape(*block)),
        [
            pltpu.VMEM((NY, *yslab), BF16), pltpu.VMEM((7, *yslab), BF16),
            pltpu.VMEM((7, *yslab), BF16),
            pltpu.VMEM((NZ, *zslab), BF16), pltpu.VMEM((7, *zslab), BF16),
            pltpu.VMEM((7, *zslab), BF16), pltpu.VMEM(zslab, F32),
            pltpu.VMEM((3, *block), BF16), pltpu.VMEM((3, *block), BF16),
            pltpu.VMEM(block, BF16), pltpu.VMEM(block, BF16),
            dma(8), dma(8), dma(7), dma(7), dma(7), dma(7), dma(8), dma(8),
            dma(8), dma(8), dma(7), dma(7), dma(3), dma(3), dma(1), dma(1),
        ],
        part, dkv, collective=1, name="reduce",
    )
    back = call(
        moe_out_kernel, shape(NE * SLAB, 128), [], full, gate, up, down, name="moe_out"
    )
    returned, kvg = call(
        return_kernel,
        (shape(NE, SLAB, 128), shape(2, TOK, 4 * HEAD)),
        [dma(NE), dma(NE), dma(3), dma(3), dma(4), dma(4), dma(2)],
        back.reshape(NE, SLAB, 128), kg, collective=2, name="return",
    )
    moe_out, input_grad, key_grad, value_grad = call(
        combine_kernel,
        (shape(TOK, 256), shape(TOK, 256), shape(TOK, 512), shape(TOK, 512)), [],
        ids, gain, returned.reshape(NE * SLAB, 128), kvg, name="combine",
    )
    return attn_out, dq, key_grad, value_grad, moe_out, input_grad


def solution(mesh):
    rows, both = P("exp", None), P("exp", "ctx")
    return jax.shard_map(
        body,
        mesh=mesh,
        in_specs=(
            both, rows, rows, both, both, both, rows, rows,
            P("exp", "ctx", None), P("exp", "ctx", None), P("exp", None, "ctx"),
        ),
        out_specs=(both, both, rows, rows, both, both),
        check_vma=False,
    )
```

time: 451 us -> 147 us (0.33)
  waiting for transfers between devices: 217 us -> 0 us
  Pallas kernels: 0 us -> 143 us
  other arithmetic: 122 us -> 0 us
  starting transfers between devices: 39.8 us -> 0 us
  matrix products: 32.8 us -> 0 us
  local copies, waits for them, and re-layouts: 21.3 us -> 2.82 us
  between operations: 16 us -> 0.66 us
    pallas_call x0 -> x8, Pallas kernels: none -> 143 us  [call(): pl.pallas_call(kernel, out_shape=outs, in_specs=specs or [vmem()] * len(a...]
    psum x1 -> x0, waiting for transfers between devices: 131 us -> none  [body(): gate_full, up_full = lax.psum((gate_part, up_part), 'ctx')]
    unnamed x4 -> x0, other arithmetic: 112 us -> none
    all_gather x3 -> x0, waiting for transfers between devices: 70 us -> none  [the longest x1 66.6 us: body(): lax.all_gather(value_pick, 'exp', axis=0, tiled=True)]
    all_to_all x5 -> x0, starting transfers between devices: 39.3 us -> none  [the longest x1 14 us: body(): lax.all_to_all(send_scaled, 'exp', split_axis=0, concat_axis=0, tiled=True)]
    dot_general x14 -> x0, matrix products: 32.8 us -> none  [the longest x1 3.67 us: body(): jnp.einsum('hrk,rhd->kd', score_grad, query_heads, preferred_element_type...]
    all_to_all x5 -> x0, waiting for transfers between devices: 15.9 us -> none  [the longest x1 6.41 us: body(): lax.all_to_all(route_in, 'exp', split_axis=0, concat_axis=0, tiled=True)]
    gather x4 -> x0, local copies, waits for them, and re-layouts: 7.08 us -> none  [the longest x2 2.97 us: body(): picked_gain = flat_gain[places]]
  transfers between devices with their start and end apart: 9 -> 0, of which waited for: 6 -> 0; matrix products, arithmetic and copies ran while one was open for 38% -> 0% of each run, Pallas kernels for 0% -> 0%
where the time goes in v1:
time: 147 us; the launch traced here: 146 us
  Pallas kernels  143 us (97%)
  local copies, waits for them, and re-layouts  2.82 us (2%)
    pallas_call x8, Pallas kernels, call(): pl.pallas_call(kernel, out_shape=outs, in_specs=specs or [vmem()] * len(a...  143 us

profile of v1, /device:TPU:1, one launch (start us, length us, event | category | flops | bytes accessed | tf_op | source)
XLA Modules:
  0.0 146.1 jit_solution(11885644388966749015)
XLA Ops:
  0.6 1.4 copy.17.ids_ref
  2.0 1.4 copy.18.gain_ref
  3.5 3.4 %prep.1 = bf16[1536,128]{1,0:T(8,128)(2,1)} custom-call(s32[128,2]{1,0:T(8,128)} %copy.17.ids_ref, f32[128,2]{1,0:T(8,128)} %copy.18.gain_ref, bf16[128,256]{1,0:T(8,128)(2,1)} %x_ref.1, bf16[128,256]{1,0:T(8,128)(2,1)} %g_ref.1), custom_call_target="tpu_custom_call" | custom-call | tf_op jit(solution)/shard_map/prep/pallas_call | solution.py:664
  6.9 43.5 %spread.1 = (bf16[2,8,4,128,128]{4,3,2,1,0:T(8,128)(2,1)}, bf16[32,48,128]{2,1,0:T(8,128)(2,1)}) custom-call(bf16[32,48,128]{2,1,0:T(8,128)(2,1)} %bitcast.5, bf16[128,512]{1,0:T(8,128)(2,1)} %key_ref.1, bf16[128,512]{1,0:T(8,128)(2,1)} %val_ref.1), custom_call_target="tpu_custom_call" | custom-call | tf_op jit(solution)/shard_map/spread/pallas_call | solution.py:664
  50.4 14.2 %attn.1 = (bf16[128,512]{1,0:T(8,128)(2,1)}, bf16[128,512]{1,0:T(8,128)(2,1)}, bf16[2,8,4,128,128]{4,3,2,1,0:T(8,128)(2,1)}) custom-call(bf16[128,512]{1,0:T(8,128)(2,1)} %q_ref.1, bf16[2,8,4,128,128]{4,3,2,1,0:T(8,128)(2,1)} %get-tuple-element.19.kv_ref, bf16[128,512]{1,0:T(8,128)(2,1)} %do_ref.1), custom_call_target="tpu_custom_call" | custom-call | tf_op jit(solution)/shard_map/attn/pallas_call | solution.py:664
  64.6 4.4 %moe_in.1.part_ref = bf16[2,8,3,48,384]{4,3,2,1,0:T(8,128)(2,1)} custom-call(bf16[1536,128]{1,0:T(8,128)(2,1)} %bitcast.6, bf16[2,256,768]{2,1,0:T(8,128)(2,1)} %gate_ref.3, bf16[2,256,768]{2,1,0:T(8,128)(2,1)} %up_ref.3, bf16[2,768,256]{2,1,0:T(8,128)(2,1)} %down_ref.3), custom_call_target="tpu_custom_call" | custom-call | tf_op jit(solution)/shard_map/moe_in/pallas_call | solution.py:664
  69.0 51.7 %reduce.1 = (bf16[2,8,3,48,384]{4,3,2,1,0:T(8,128)(2,1)}, bf16[128,128]{1,0:T(8,128)(2,1)}) custom-call(bf16[2,8,3,48,384]{4,3,2,1,0:T(8,128)(2,1)} %moe_in.1.part_ref, bf16[2,8,4,128,128]{4,3,2,1,0:T(8,128)(2,1)} %get-tuple-element.23.dkv_ref), custom_call_target="tpu_custom_call" | custom-call | tf_op jit(solution)/shard_map/reduce/pallas_call | solution.py:664
  120.7 4.4 %moe_out.1 = bf16[1536,128]{1,0:T(8,128)(2,1)} custom-call(bf16[2,8,3,48,384]{4,3,2,1,0:T(8,128)(2,1)} %get-tuple-element.24.full_ref, bf16[2,256,768]{2,1,0:T(8,128)(2,1)} %gate_ref.3, bf16[2,256,768]{2,1,0:T(8,128)(2,1)} %up_ref.3, bf16[2,768,256]{2,1,0:T(8,128)(2,1)} %down_ref.3), custom_call_target="tpu_custom_call" | custom-call | tf_op jit(solution)/shard_map/moe_out/pallas_call | solution.py:664
  125.1 17.9 %return.1 = (bf16[32,48,128]{2,1,0:T(8,128)(2,1)}, bf16[2,128,512]{2,1,0:T(8,128)(2,1)}) custom-call(bf16[32,48,128]{2,1,0:T(8,128)(2,1)} %bitcast.4, bf16[128,128]{1,0:T(8,128)(2,1)} %get-tuple-element.25.kg_ref), custom_call_target="tpu_custom_call" | custom-call | tf_op jit(solution)/shard_map/return/pallas_call | solution.py:664
  142.9 3.2 %combine.1 = (bf16[128,256]{1,0:T(8,128)(2,1)}, bf16[128,256]{1,0:T(8,128)(2,1)}, bf16[128,512]{1,0:T(8,128)(2,1)}, bf16[128,512]{1,0:T(8,128)(2,1)}) custom-call(s32[128,2]{1,0:T(8,128)} %copy.17.ids_ref, f32[128,2]{1,0:T(8,128)} %copy.18.gain_ref, bf16[1536,128]{1,0:T(8,128)(2,1)} %bitcast.7, bf16[2,128,512]{2,1,0:T(8,128)(2,1)} %get-tuple-element.27.kvg_ref), custom_call_target="tpu_custom_call" | custom-call | tf_op jit(solution)/shard_map/combine/pallas_call | solution.py:664

commit v2 on v0

v2 whole, which is shorter than its diff:
```python
import functools

import jax
import jax.numpy as jnp
from jax import lax
from jax.experimental import pallas as pl
from jax.experimental.pallas import tpu as pltpu
from jax.sharding import PartitionSpec as P

MESH = pl.DeviceIdType.MESH
F32 = jnp.float32
BF16 = jnp.bfloat16
HEAD = 128
NX, NZ, NY = 4, 8, 8
NE = NX * NZ
TOK = 128
LOCAL = 2
EXPERTS = LOCAL * NE
SLOT = 6
GROUP = LOCAL * SLOT
SLAB = 4 * GROUP
ROWS = NE * GROUP
FF = 768
HALF = FF // 2
YROWS = ROWS // NY
SCALE = HEAD ** (-0.5)
VMEM_LIMIT = 60 * 1024 * 1024


def dot(a, b):
    return jnp.dot(a, b, preferred_element_type=F32)


def dot_t(a, b):
    return lax.dot_general(a, b, (((1,), (1,)), ((), ())), preferred_element_type=F32)


def t_dot(a, b):
    return lax.dot_general(a, b, (((0,), (0,)), ((), ())), preferred_element_type=F32)


def fdiv(a, n):
    return jnp.floor((a + 0.5) * (1.0 / n))


def fiota(shape, dim):
    return lax.broadcasted_iota(jnp.int32, shape, dim).astype(F32)


def column(row):
    return jnp.broadcast_to(row, (TOK, TOK)).T


def route_tables(ids):
    lane = fiota((TOK, EXPERTS), 1)
    ids = ids.astype(F32)
    first = jnp.where(column(ids[0:1])[:, :EXPERTS] == lane, 1.0, 0.0)
    second = jnp.where(column(ids[1:2])[:, :EXPERTS] == lane, 1.0, 0.0)
    row = lax.broadcasted_iota(jnp.int32, (TOK, TOK), 0)
    col = lax.broadcasted_iota(jnp.int32, (TOK, TOK), 1)
    before = jnp.where(col < row, 1.0, 0.0).astype(BF16)
    place = dot(before, (first + second).astype(BF16)) + 1.0
    return (first * place).astype(BF16), (second * place).astype(BF16)


def slab_index(p):
    dest = fdiv(p, SLAB)
    inner = p - dest * SLAB
    quarter = fdiv(inner, GROUP)
    inner = inner - quarter * GROUP
    local = fdiv(inner, SLOT)
    slot = inner - local * SLOT
    return dest * LOCAL + local, quarter, slot


def prepare(ids_ref, gain_ref, x_ref, g_ref, out_ref):
    v0, v1 = route_tables(ids_ref[...])
    total = NE * SLAB
    expert, quarter, slot = slab_index(fiota((total, 1), 0))
    pick = jnp.where(expert == fiota((total, EXPERTS), 1), 1.0, 0.0).astype(BF16)
    y0 = dot_t(pick, v0)
    y1 = dot_t(pick, v1)
    want = slot + 1.0
    hit0 = jnp.where(y0 == want, 1.0, 0.0)
    hit1 = jnp.where(y1 == want, 1.0, 0.0)
    both = hit0 + hit1
    q = [jnp.where(quarter == float(i), 1.0, 0.0) for i in range(4)]
    table = jnp.concatenate(
        [both * q[0], both * q[1], hit0 * q[2], hit0 * q[3], hit1 * q[2], hit1 * q[3]], axis=1
    ).astype(BF16)
    x = x_ref[...]
    g = g_ref[...].astype(F32)
    gain = gain_ref[...]
    w0, w1 = column(gain[0:1]), column(gain[1:2])
    lo, hi = g[:, :128], g[:, 128:]
    scaled = [(a * w).astype(BF16) for w in (w0, w1) for a in (lo, hi)]
    rows = jnp.concatenate([x[:, :128], x[:, 128:]] + scaled, axis=0)
    out_ref[...] = dot(table, rows).astype(BF16).reshape(NE, SLAB, 128)


def combine_kernel(
    ids_ref, gain_ref, back_ref, kvg_ref, ao_ref, dq_ref,
    out_ref, in_ref, kg_ref, vg_ref, ao_out, dq_out,
):
    v0, v1 = route_tables(ids_ref[...])
    total = NE * SLAB
    expert, quarter, slot = slab_index(fiota((1, total), 1))
    pick = jnp.where(expert == fiota((EXPERTS, total), 0), 1.0, 0.0).astype(BF16)
    y0 = dot(v0, pick)
    y1 = dot(v1, pick)
    want = slot + 1.0
    hit0 = jnp.where(y0 == want, 1.0, 0.0)
    hit1 = jnp.where(y1 == want, 1.0, 0.0)
    both = hit0 + hit1
    q = [jnp.where(quarter == float(i), 1.0, 0.0) for i in range(4)]
    back = back_ref[...]
    gain = gain_ref[...]
    w0, w1 = column(gain[0:1]), column(gain[1:2])
    for i in range(2):
        part0 = dot((hit0 * q[i]).astype(BF16), back)
        part1 = dot((hit1 * q[i]).astype(BF16), back)
        out_ref[:, i * 128 : (i + 1) * 128] = (part0 * w0 + part1 * w1).astype(BF16)
        in_ref[:, i * 128 : (i + 1) * 128] = dot((both * q[2 + i]).astype(BF16), back).astype(BF16)
    kg_ref[...] = kvg_ref[0]
    vg_ref[...] = kvg_ref[1]
    ao_out[...] = ao_ref[...]
    dq_out[...] = dq_ref[...]


PACK = 8 * GROUP


def pack_table(transposed):
    n = 4 * PACK
    shape = (n, n)
    r = fiota((1, n) if transposed else (n, 1), 1 if transposed else 0)
    quarter = fdiv(r, PACK)
    inner = r - quarter * PACK
    source = fdiv(inner, GROUP)
    p = source * SLAB + quarter * GROUP + (inner - source * GROUP)
    return jnp.where(p == fiota(shape, 0 if transposed else 1), 1.0, 0.0).astype(BF16)


def first_local(rows):
    r = fiota((rows, 1), 0)
    inner = r - fdiv(r, GROUP) * GROUP
    return inner < float(SLOT)


class Place:
    def __init__(self):
        self.e = lax.axis_index("exp")
        self.c = lax.axis_index("ctx")
        self.z, self.x = self.e // NX, self.e % NX
        self.y, self.k = self.c // 2, self.c % 2
        self.sgn = 1 - 2 * self.k
        self.mate = {"exp": self.e, "ctx": self.y * 2 + 1 - self.k}
        self.twin = {"exp": self.e, "ctx": (self.y + 1 - 2 * (self.y % 2)) * 2 + self.k}

    def at_z(self, step):
        return (self.z + self.sgn * step + 2 * NZ) % NZ

    def at_x(self, step):
        return (self.x + self.sgn * step + 2 * NX) % NX

    def at_y(self, step):
        return (self.y + self.sgn * step + 2 * NY) % NY

    def dev_z(self, step):
        return {"exp": self.at_z(step) * NX + self.x, "ctx": self.c}

    def dev_x(self, step):
        return {"exp": self.z * NX + self.at_x(step), "ctx": self.c}

    def dev_y(self, step):
        return {"exp": self.e, "ctx": self.at_y(step) * 2 + self.k}


def remote(src, dst, send, recv, device):
    return pltpu.make_async_remote_copy(
        src_ref=src, dst_ref=dst, send_sem=send, recv_sem=recv, device_id=device,
        device_id_type=MESH,
    )


def exchange(here, send_ref, recv_ref, send_sem, recv_sem):
    def desc(o):
        dest = (here.e + o) % NE
        return remote(
            send_ref.at[dest], recv_ref.at[here.e], send_sem.at[o], recv_sem.at[o],
            {"exp": dest, "ctx": here.c},
        )

    def incoming(o):
        source = (here.e + NE - o) % NE
        return remote(
            send_ref.at[source], recv_ref.at[source], send_sem.at[o], recv_sem.at[o],
            {"exp": source, "ctx": here.c},
        )

    def begin(first, last):
        def go(o, carry):
            desc(o).start()
            return carry

        lax.fori_loop(first, last, go, 0)

    def finish():
        def go(o, carry):
            desc(o).wait_send()
            incoming(o).wait_recv()
            return carry

        lax.fori_loop(1, NE, go, 0)

    return begin, finish


def add16(*refs):
    total = refs[0].astype(F32)
    for r in refs[1:]:
        total = total + r.astype(F32)
    return total


ORDER = [4, -3, 3, -2, 2, -1, 1, 0]
DEEP = NZ // 2
KEYS = NX * TOK


def layer_kernel(
    ids_ref, gain_ref, x_ref, g_ref, key_ref, val_ref, q_hbm, do_hbm, gate_hbm, up_hbm, down_hbm,
    ao_ref, dq_ref, ret_ref, kvg_ref,
    q_ref, do_ref, gate_ref, up_ref, down_ref,
    send, recv, rows_ref, part, pmate, ysend, yrecv, full,
    kv, qs, dos, e_ref, mj, m_ref, l_ref, o_ref, d_ref, dq_acc,
    dkv, dmate, zsend, zrecv, own4, xsend, xrecv, tsend, trecv, kg, back,
    s_in, s_l, s_far, r_far, s_kx, r_kx, s_kz, r_kz, s_km, r_km,
    s_pm, r_pm, s_y, r_y, s_g, r_g, s_gm, r_gm,
    s_dm, r_dm, s_z, r_z, s_x, r_x, s_t, r_t, s_c, r_c, s_cm, r_cm, s_ret, r_ret,
):
    here = Place()
    k, z, x, e = here.k, here.z, here.x, here.e
    barrier = pltpu.get_barrier_semaphore()

    def greet(device):
        pl.semaphore_signal(barrier, inc=1, device_id=device, device_id_type=MESH)

    near = [here.mate] + [here.dev_y(s) for s in (1, -1, 2, -2, 4)]
    for device in near:
        greet(device)

    def greet_far(o, carry):
        greet({"exp": (e + o) % NE, "ctx": here.c})
        return carry

    lax.fori_loop(1, NE, greet_far, 0)

    loads = [
        pltpu.make_async_copy(a, b, s_in.at[i])
        for i, (a, b) in enumerate(
            [(gate_hbm, gate_ref), (up_hbm, up_ref), (down_hbm, down_ref), (q_hbm, q_ref), (do_hbm, do_ref)]
        )
    ]
    for c in loads:
        c.start()
    cols = pl.ds(pl.multiple_of((here.y // 2) * HEAD, HEAD), HEAD)
    own = kv.at[k, z, x]

    @pl.when(k == 0)
    def _():
        pltpu.make_async_copy(key_ref.at[:, cols], own, s_l.at[0]).start()

    @pl.when(k == 1)
    def _():
        pltpu.make_async_copy(val_ref.at[:, cols], own, s_l.at[0]).start()

    prepare(ids_ref, gain_ref, x_ref, g_ref, send)
    pltpu.make_async_copy(key_ref.at[:, cols], own, s_l.at[0]).wait()
    pl.semaphore_wait(barrier, len(near) + NE - 1)

    sends = []

    def go(c):
        c.start()
        sends.append(c)

    begin, finish = exchange(here, send, recv, s_far, r_far)
    begin(1, NE)
    local = pltpu.make_async_copy(send.at[e], recv.at[e], s_l.at[1])
    local.start()

    def block(step):
        return kv.at[k, z, here.at_x(step)]

    def slab(step):
        return kv.at[k, here.at_z(step)]

    def xcopy(i, origin, to):
        return remote(block(origin), block(origin), s_kx.at[i], r_kx.at[i], here.dev_x(to))

    def zcopy(i, origin, to):
        return remote(slab(origin), slab(origin), s_kz.at[i], r_kz.at[i], here.dev_z(to))

    def kv_mate(i, origin):
        return remote(slab(origin), slab(origin), s_km.at[i], r_km.at[i], here.mate)

    go(xcopy(0, 0, 1))
    go(xcopy(2, 0, -1))
    xcopy(0, -1, 1).wait_recv()
    go(xcopy(1, -1, 1))
    xcopy(2, 1, -1).wait_recv()
    xcopy(1, -2, 1).wait_recv()
    go(zcopy(0, 0, 1))
    go(zcopy(DEEP, 0, -1))
    go(kv_mate(0, 0))

    def kv_step(s):
        zcopy(s - 1, -s, 1).wait_recv()
        if s < DEEP:
            go(zcopy(s, -s, 1))
        go(kv_mate(s, -s))
        if s < DEEP:
            zcopy(DEEP + s - 1, s, -1).wait_recv()
            if s < DEEP - 1:
                go(zcopy(DEEP + s, s, -1))
            go(kv_mate(DEEP + s, s))

    def kv_from_mate(i, step):
        spot = kv.at[1 - k, here.at_z(step)]
        remote(spot, spot, s_km.at[i], r_km.at[i], here.mate).wait_recv()

    def kv_ready(d):
        kv_from_mate(d, d)
        if 0 < d < DEEP:
            kv_from_mate(DEEP + d, -d)

    for c in loads:
        c.wait()
    local.wait()
    finish()

    table = pack_table(False)
    n = 4 * PACK
    for g in range(NE // 8):
        slabs = recv[g * 8 : (g + 1) * 8].reshape(n, 128)
        packed = dot(table, slabs).astype(BF16)
        for i in range(4):
            rows_ref[i // 2, g * PACK : (g + 1) * PACK, (i % 2) * 128 : (i % 2 + 1) * 128] = packed[
                i * PACK : (i + 1) * PACK, :
            ]
    first = first_local(ROWS)

    def product(m):
        if m < 2:
            w_ref = (gate_ref, up_ref)[m]
            rows = rows_ref[0]
            whole = jnp.where(first, dot(rows, w_ref[0]), dot(rows, w_ref[1]))
        else:
            rows = rows_ref[1]
            whole = jnp.where(first, dot_t(rows, down_ref[0]), dot_t(rows, down_ref[1]))
        whole = whole.astype(BF16)
        for c in range(2):
            for y in range(NY):
                part[c, y, m] = whole[y * YROWS : (y + 1) * YROWS, c * HALF : (c + 1) * HALF]
        for i, step in enumerate(ORDER):
            d = here.at_y(-step)
            j = m * 8 + i
            go(remote(part.at[1 - k, d, m], pmate.at[d, m], s_pm.at[j], r_pm.at[j], here.mate))

    def part_in(i, m):
        d = here.at_y(ORDER[i])
        j = m * 8 + i
        remote(part.at[k, d, m], pmate.at[d, m], s_pm.at[j], r_pm.at[j], here.mate).wait_recv()
        return d

    def yslot(i, m, to):
        j = m * 7 + i
        return remote(ysend.at[j], yrecv.at[j], s_y.at[j], r_y.at[j], here.dev_y(to))

    def y_step(s, m):
        d = part_in(ORDER.index(DEEP - s), m)
        j = m * 7 + s
        if s == 0:
            ysend[j] = add16(part[k, d, m], pmate[d, m]).astype(BF16)
        else:
            yslot(s - 1, m, 1).wait_recv()
            ysend[j] = add16(part[k, d, m], pmate[d, m], yrecv[j - 1]).astype(BF16)
        go(yslot(s, m, 1))
        if s < DEEP - 1:
            d = part_in(ORDER.index(s + 1 - DEEP), m)
            j = m * 7 + DEEP + s
            if s == 0:
                ysend[j] = add16(part[k, d, m], pmate[d, m]).astype(BF16)
            else:
                yslot(DEEP + s - 1, m, -1).wait_recv()
                ysend[j] = add16(part[k, d, m], pmate[d, m], yrecv[j - 1]).astype(BF16)
            go(yslot(DEEP + s, m, -1))

    def gcopy(i, m, origin, to):
        spot = full.at[k, here.at_y(origin), m]
        j = m * 7 + i
        return remote(spot, spot, s_g.at[j], r_g.at[j], here.dev_y(to))

    def g_mate(i, m, origin):
        spot = full.at[k, here.at_y(origin), m]
        j = m * 8 + i
        return remote(spot, spot, s_gm.at[j], r_gm.at[j], here.mate)

    def activate():
        total = []
        for m in range(3):
            d = part_in(ORDER.index(0), m)
            yslot(2 * DEEP - 2, m, -1).wait_recv()
            yslot(DEEP - 1, m, 1).wait_recv()
            total.append(
                add16(part[k, d, m], pmate[d, m], yrecv[m * 7 + 2 * DEEP - 2], yrecv[m * 7 + DEEP - 1])
            )
        gate, up, hidden_grad = total
        sig = 1.0 / (1.0 + jnp.exp(-gate))
        act = gate * sig
        full[k, here.y, 0] = (act * up).astype(BF16)
        full[k, here.y, 1] = (hidden_grad * up * sig * (1.0 + gate * (1.0 - sig))).astype(BF16)
        full[k, here.y, 2] = (hidden_grad * act).astype(BF16)
        for m in range(3):
            go(gcopy(0, m, 0, 1))
            go(gcopy(DEEP, m, 0, -1))
        for m in range(3):
            go(g_mate(0, m, 0))

    def gather_step(s):
        for m in range(3):
            gcopy(s - 1, m, -s, 1).wait_recv()
            if s < DEEP:
                go(gcopy(s, m, -s, 1))
            go(g_mate(s, m, -s))
            if s < DEEP:
                gcopy(DEEP + s - 1, m, s, -1).wait_recv()
                if s < DEEP - 1:
                    go(gcopy(DEEP + s, m, s, -1))
                go(g_mate(DEEP + s, m, s))

    def gather_from_mate():
        for m in range(3):
            pairs = [(s, s) for s in range(DEEP + 1)] + [(DEEP + s, -s) for s in range(1, DEEP)]
            for i, step in pairs:
                spot = full.at[1 - k, here.at_y(step), m]
                j = m * 8 + i
                remote(spot, spot, s_gm.at[j], r_gm.at[j], here.mate).wait_recv()

    heads = q_ref.shape[1] // HEAD
    width = heads * TOK

    def stack():
        for h in range(heads):
            qs[h * TOK : (h + 1) * TOK, :] = q_ref[:, h * HEAD : (h + 1) * HEAD]
            dos[h * TOK : (h + 1) * TOK, :] = do_ref[:, h * HEAD : (h + 1) * HEAD]
        m_ref[...] = jnp.full((1, width), -jnp.inf, F32)
        l_ref[...] = jnp.zeros((1, width), F32)
        o_ref[...] = jnp.zeros((HEAD, width), F32)
        dq_acc[...] = jnp.zeros((HEAD, width), F32)

    def forward(step):
        j = here.at_z(step)
        lane = lax.broadcasted_iota(jnp.int32, (1, width), 1)
        q_pos = e * TOK + jnp.bitwise_and(lane, TOK - 1)
        row = lax.broadcasted_iota(jnp.int32, (KEYS, 1), 0) + j * KEYS
        s = dot_t(kv[0, j].reshape(KEYS, HEAD), qs[...]) * SCALE
        s = jnp.where(row <= q_pos, s, -jnp.inf)
        old = m_ref[...]
        m = jnp.maximum(old, jnp.max(s, axis=0, keepdims=True))
        p = jnp.exp(s - m)
        p16 = p.astype(BF16)
        e_ref[j] = p16
        mj[j] = m
        m_ref[...] = m
        fade = jnp.exp(old - m)
        l_ref[...] = l_ref[...] * fade + jnp.sum(p, axis=0, keepdims=True)
        o_ref[...] = o_ref[...] * fade + t_dot(kv[1, j].reshape(KEYS, HEAD), p16)

    def normalize():
        inv = 1.0 / l_ref[...]
        l_ref[...] = inv
        o16 = (o_ref[...] * inv).astype(BF16)
        turned = o16.astype(F32).T
        for h in range(heads):
            ao_ref[:, h * HEAD : (h + 1) * HEAD] = turned[h * TOK : (h + 1) * TOK, :].astype(BF16)
        do_t = dos[...].astype(F32).T
        d_ref[...] = jnp.sum(do_t * o16.astype(F32), axis=0, keepdims=True)

    def backward(step):
        j = here.at_z(step)
        keys = kv[0, j].reshape(KEYS, HEAD)
        dp = dot_t(kv[1, j].reshape(KEYS, HEAD), dos[...])
        p = e_ref[j].astype(F32) * (jnp.exp(mj[j] - m_ref[...]) * l_ref[...])
        ds = (p * (dp - d_ref[...])).astype(BF16)
        dkv[0, j] = (dot(ds, qs[...]) * SCALE).astype(BF16).reshape(NX, TOK, HEAD)
        dkv[1, j] = dot(p.astype(BF16), dos[...]).astype(BF16).reshape(NX, TOK, HEAD)
        dq_acc[...] += t_dot(keys, ds)
        i = ORDER.index(step if step == DEEP else -step)
        go(remote(dkv.at[1 - k, j], dmate.at[j], s_dm.at[i], r_dm.at[i], here.mate))

    def query_grad():
        turned = (dq_acc[...] * SCALE).T
        for h in range(heads):
            dq_ref[:, h * HEAD : (h + 1) * HEAD] = turned[h * TOK : (h + 1) * TOK, :].astype(BF16)

    def dkv_in(i):
        d = here.at_z(ORDER[i])
        remote(dkv.at[k, d], dmate.at[d], s_dm.at[i], r_dm.at[i], here.mate).wait_recv()
        return d

    def zslot(i, to):
        return remote(zsend.at[i], zrecv.at[i], s_z.at[i], r_z.at[i], here.dev_z(to))

    def z_step(s):
        d = dkv_in(ORDER.index(DEEP - s))
        if s == 0:
            zsend[0] = add16(dkv[k, d], dmate[d]).astype(BF16)
        else:
            zslot(s - 1, 1).wait_recv()
            zsend[s] = add16(dkv[k, d], dmate[d], zrecv[s - 1]).astype(BF16)
        go(zslot(s, 1))
        if s < DEEP - 1:
            d = dkv_in(ORDER.index(s + 1 - DEEP))
            i = DEEP + s
            if s == 0:
                zsend[i] = add16(dkv[k, d], dmate[d]).astype(BF16)
            else:
                zslot(i - 1, -1).wait_recv()
                zsend[i] = add16(dkv[k, d], dmate[d], zrecv[i - 1]).astype(BF16)
            go(zslot(i, -1))

    def xslot(i, to):
        return remote(xsend.at[i], xrecv.at[i], s_x.at[i], r_x.at[i], here.dev_x(to))

    def x_first():
        d = dkv_in(ORDER.index(0))
        zslot(2 * DEEP - 2, -1).wait_recv()
        zslot(DEEP - 1, 1).wait_recv()
        own4[...] = add16(dkv[k, d], dmate[d], zrecv[2 * DEEP - 2], zrecv[DEEP - 1])
        xsend[0] = own4[here.at_x(2)].astype(BF16)
        go(xslot(0, 1))
        xsend[2] = own4[here.at_x(-1)].astype(BF16)
        go(xslot(2, -1))

    def x_second():
        xslot(0, 1).wait_recv()
        xsend[1] = add16(own4[here.at_x(1)], xrecv[0]).astype(BF16)
        go(xslot(1, 1))

    twin = remote(tsend, trecv, s_t.at[0], r_t.at[0], here.twin)

    def x_third():
        xslot(2, -1).wait_recv()
        xslot(1, 1).wait_recv()
        tsend[...] = add16(own4[x], xrecv[2], xrecv[1]).astype(BF16)
        go(twin)

    def spot(which, step):
        head = here.at_y(step) // 2
        return kvg_ref.at[which, :, pl.ds(pl.multiple_of(head * HEAD, HEAD), HEAD)]

    mine = pltpu.make_async_copy(kg, spot(k, 0), s_l.at[2])

    def spread():
        twin.wait_recv()
        kg[...] = add16(tsend[...], trecv[...]).astype(BF16)
        for i, step in enumerate((2, 4, 6)):
            go(remote(kg, spot(k, 0), s_c.at[i], r_c.at[i], here.dev_y(step)))
        go(remote(kg, spot(k, 0), s_cm.at[3], r_cm.at[3], here.mate))
        mine.start()

    def spread_end():
        for i, step in enumerate((2, 4, 6)):
            remote(kg, spot(k, -step), s_c.at[i], r_c.at[i], here.dev_y(-step)).wait_recv()
            go(remote(spot(k, -step), spot(k, -step), s_cm.at[i], r_cm.at[i], here.mate))
        for i, step in enumerate((2, 4, 6)):
            there = spot(1 - k, step)
            remote(there, there, s_cm.at[i], r_cm.at[i], here.mate).wait_recv()
        remote(kg, spot(1 - k, 0), s_cm.at[3], r_cm.at[3], here.mate).wait_recv()
        mine.wait()

    ret_begin, ret_finish = exchange(here, back, ret_ref, s_ret, r_ret)
    ret_local = pltpu.make_async_copy(back.at[e], ret_ref.at[e], s_l.at[3])

    def experts_out():
        def both(m, weight, transposed):
            halves = [full[c, :, m].reshape(ROWS, HALF) for c in range(2)]
            whole = jnp.concatenate(halves, axis=1)
            f = dot_t if transposed else dot
            return jnp.where(first, f(whole, weight[0]), f(whole, weight[1]))

        route_out = both(0, down_ref, False).astype(BF16)
        route_in = (both(1, gate_ref, True) + both(2, up_ref, True)).astype(BF16)
        quarters = [route_out[:, :128], route_out[:, 128:], route_in[:, :128], route_in[:, 128:]]
        unpack = pack_table(True)
        for g in range(NE // 8):
            stacked = jnp.concatenate([q[g * PACK : (g + 1) * PACK] for q in quarters], axis=0)
            back[g * 8 : (g + 1) * 8] = dot(unpack, stacked).astype(BF16).reshape(8, SLAB, 128)
        ret_begin(1, NE)
        ret_local.start()

    product(0)
    kv_step(1)
    product(1)
    y_step(0, 0)
    product(2)
    y_step(0, 1)
    kv_step(2)
    y_step(0, 2)
    stack()
    kv_ready(0)
    forward(0)
    for m in range(3):
        y_step(1, m)
    kv_step(3)
    kv_ready(1)
    forward(-1)
    forward(1)
    for m in range(3):
        y_step(2, m)
    kv_step(4)
    kv_ready(2)
    forward(-2)
    forward(2)
    for m in range(3):
        y_step(3, m)
    kv_ready(3)
    forward(-3)
    forward(3)
    activate()
    kv_ready(4)
    forward(4)
    normalize()
    gather_step(1)
    backward(4)
    backward(-3)
    gather_step(2)
    backward(3)
    z_step(0)
    backward(-2)
    gather_step(3)
    backward(2)
    z_step(1)
    backward(-1)
    gather_step(4)
    gather_from_mate()
    experts_out()
    backward(1)
    z_step(2)
    backward(0)
    z_step(3)
    query_grad()
    x_first()
    x_second()
    x_third()
    spread()
    spread_end()
    ret_finish()
    ret_local.wait()
    for c in sends:
        c.wait_send()


def vmem():
    return pl.BlockSpec(memory_space=pltpu.VMEM)


def dma(n):
    return pltpu.SemaphoreType.DMA((n,))


def call(kernel, outs, scratch, *args, specs=None, collective=None, name=None, flops=0):
    params = {"vmem_limit_bytes": VMEM_LIMIT}
    if collective is not None:
        params.update(collective_id=collective, has_side_effects=True)
    return pl.pallas_call(
        kernel,
        out_shape=outs,
        in_specs=specs or [vmem()] * len(args),
        out_specs=jax.tree.map(lambda o: vmem(), outs),
        scratch_shapes=scratch,
        compiler_params=pltpu.CompilerParams(**params),
        name=name,
    )(*args)


def shape(*dims, dtype=BF16):
    return jax.ShapeDtypeStruct(dims, dtype)


def body(q, key, val, do, x, g, ids, gain, gate, up, down):
    ids, gain = ids.T, gain.T
    hbm = pl.BlockSpec(memory_space=pl.ANY)
    heads = q.shape[1] // HEAD
    width = heads * TOK
    yslab, zslab, block = (YROWS, HALF), (NX, TOK, HEAD), (TOK, HEAD)

    def f32(*dims):
        return pltpu.VMEM(dims, F32)

    def b16(*dims):
        return pltpu.VMEM(dims, BF16)

    sems = [5, 4, NE, NE, 3, 3, 8, 8, 8, 8, 24, 24, 21, 21, 21, 21, 24, 24]
    sems += [8, 8, 7, 7, 3, 3, 1, 1, 3, 3, 4, 4, NE, NE]
    attn_out, dq, returned, kvg = call(
        layer_kernel,
        (shape(*q.shape), shape(*q.shape), shape(NE, SLAB, 128), shape(2, TOK, 4 * HEAD)),
        [
            b16(*q.shape), b16(*do.shape), b16(*gate.shape), b16(*up.shape), b16(*down.shape),
            b16(NE, SLAB, 128), b16(NE, SLAB, 128), b16(2, ROWS, 256),
            b16(2, NY, 3, *yslab), b16(NY, 3, *yslab), b16(21, *yslab), b16(21, *yslab),
            b16(2, NY, 3, *yslab),
            b16(2, NZ, *zslab), b16(width, HEAD), b16(width, HEAD), b16(NZ, KEYS, width),
            f32(NZ, 1, width), f32(1, width), f32(1, width), f32(HEAD, width), f32(1, width),
            f32(HEAD, width),
            b16(2, NZ, *zslab), b16(NZ, *zslab), b16(7, *zslab), b16(7, *zslab), f32(*zslab),
            b16(3, *block), b16(3, *block), b16(*block), b16(*block), b16(*block),
            b16(NE, SLAB, 128),
        ]
        + [dma(n) for n in sems],
        ids, gain, x, g, key, val, q, do, gate, up, down,
        specs=[vmem()] * 4 + [hbm] * 7, collective=0, name="layer",
    )
    moe_out, input_grad, key_grad, value_grad, attn_out, dq = call(
        combine_kernel,
        (shape(TOK, 256), shape(TOK, 256), shape(TOK, 512), shape(TOK, 512),
         shape(*q.shape), shape(*q.shape)), [],
        ids, gain, returned.reshape(NE * SLAB, 128), kvg, attn_out, dq, name="combine",
    )
    return attn_out, dq, key_grad, value_grad, moe_out, input_grad


def solution(mesh):
    rows, both = P("exp", None), P("exp", "ctx")
    return jax.shard_map(
        body,
        mesh=mesh,
        in_specs=(
            both, rows, rows, both, both, both, rows, rows,
            P("exp", "ctx", None), P("exp", "ctx", None), P("exp", None, "ctx"),
        ),
        out_specs=(both, both, rows, rows, both, both),
        check_vma=False,
    )
```

time: 451 us -> 110 us (0.24)
  waiting for transfers between devices: 217 us -> 0 us
  other arithmetic: 122 us -> 0 us
  Pallas kernels: 0 us -> 109 us
  starting transfers between devices: 39.8 us -> 0 us
  matrix products: 32.8 us -> 0 us
  local copies, waits for them, and re-layouts: 21.3 us -> 0 us
  between operations: 16 us -> 0.64 us
    psum x1 -> x0, waiting for transfers between devices: 131 us -> none  [body(): gate_full, up_full = lax.psum((gate_part, up_part), 'ctx')]
    unnamed x4 -> x0, other arithmetic: 112 us -> none
    pallas_call x0 -> x2, Pallas kernels: none -> 109 us  [call(): pl.pallas_call(kernel, out_shape=outs, in_specs=specs or [vmem()] * len(a...]
    all_gather x3 -> x0, waiting for transfers between devices: 70 us -> none  [the longest x1 66.6 us: body(): lax.all_gather(value_pick, 'exp', axis=0, tiled=True)]
    all_to_all x5 -> x0, starting transfers between devices: 39.3 us -> none  [the longest x1 14 us: body(): lax.all_to_all(send_scaled, 'exp', split_axis=0, concat_axis=0, tiled=True)]
    dot_general x14 -> x0, matrix products: 32.8 us -> none  [the longest x1 3.67 us: body(): jnp.einsum('hrk,rhd->kd', score_grad, query_heads, preferred_element_type...]
    all_to_all x5 -> x0, waiting for transfers between devices: 15.9 us -> none  [the longest x1 6.41 us: body(): lax.all_to_all(route_in, 'exp', split_axis=0, concat_axis=0, tiled=True)]
    gather x4 -> x0, local copies, waits for them, and re-layouts: 7.08 us -> none  [the longest x2 2.97 us: body(): picked_gain = flat_gain[places]]
  transfers between devices with their start and end apart: 9 -> 0, of which waited for: 6 -> 0; matrix products, arithmetic and copies ran while one was open for 38% -> 0% of each run, Pallas kernels for 0% -> 0%
where the time goes in v2:
time: 110 us
  Pallas kernels  109 us (99%)
    pallas_call x2, Pallas kernels, call(): pl.pallas_call(kernel, out_shape=outs, in_specs=specs or [vmem()] * len(a...  109 us

profile of v2, /device:TPU:1, one launch (start us, length us, event | category | flops | bytes accessed | tf_op | source)
XLA Modules:
  0.0 109.7 jit_solution(8006868689606552501)
XLA Ops:
  0.6 105.9 %layer.1 = (bf16[128,512]{1,0:T(8,128)(2,1)}, bf16[128,512]{1,0:T(8,128)(2,1)}, bf16[32,48,128]{2,1,0:T(8,128)(2,1)}, bf16[2,128,512]{2,1,0:T(8,128)(2,1)}) custom-call(s32[2,128]{1,0:T(2,128)} %bitcast.4, f32[2,128]{1,0:T(2,128)} %bitcast.6, bf16[128,256]{1,0:T(8,128)(2,1)} %x_ref.1, bf16[128,256]{1,0:T(8,128)(2,1)} %g_ref.1, bf16[128,512]{1,0:T(8,128)(2,1)} %key_ref.1, ...), custom_call_target="tpu_custom_call" | custom-call | tf_op jit(solution)/shard_map/layer/pallas_call | solution.py:678
  106.5 3.2 %combine.1 = (bf16[128,256]{1,0:T(8,128)(2,1)}, bf16[128,256]{1,0:T(8,128)(2,1)}, bf16[128,512]{1,0:T(8,128)(2,1)}, bf16[128,512]{1,0:T(8,128)(2,1)}, bf16[128,5...) custom-call(s32[2,128]{1,0:T(2,128)} %bitcast.5, f32[2,128]{1,0:T(2,128)} %bitcast.7, bf16[1536,128]{1,0:T(8,128)(2,1)} %bitcast.3, ...), custom_call_target="tpu_custom_call" | custom-call | tf_op jit(solution)/shard_map/combine/pallas_call | solution.py:678

commit v3 on v2

--- a/solution.py
+++ b/solution.py
@@ -130,21 +130,24 @@
 PACK = 8 * GROUP
 
 
-def pack_table(transposed):
-    n = 4 * PACK
-    shape = (n, n)
+def pack_table(transposed, rows):
+    n = 4 * rows
     r = fiota((1, n) if transposed else (n, 1), 1 if transposed else 0)
-    quarter = fdiv(r, PACK)
-    inner = r - quarter * PACK
+    quarter = fdiv(r, rows)
+    inner = r - quarter * rows
     source = fdiv(inner, GROUP)
     p = source * SLAB + quarter * GROUP + (inner - source * GROUP)
-    return jnp.where(p == fiota(shape, 0 if transposed else 1), 1.0, 0.0).astype(BF16)
+    return jnp.where(p == fiota((n, n), 0 if transposed else 1), 1.0, 0.0).astype(BF16)
 
 
 def first_local(rows):
     r = fiota((rows, 1), 0)
     inner = r - fdiv(r, GROUP) * GROUP
     return inner < float(SLOT)
+
+
+def source(y, i):
+    return ((y - 2 * i + 2 * NZ) % NZ) * NX + i
 
 
 class Place:
@@ -183,7 +186,7 @@
     )
 
 
-def exchange(here, send_ref, recv_ref, send_sem, recv_sem):
+def exchange(here, send_ref, recv_ref, send_sem, recv_sem, single=False):
     def desc(o):
         dest = (here.e + o) % NE
         return remote(
@@ -213,7 +216,7 @@
 
         lax.fori_loop(1, NE, go, 0)
 
-    return begin, finish
+    return (desc if single else begin), finish
 
 
 def add16(*refs):
@@ -224,8 +227,18 @@
 
 
 ORDER = [4, -3, 3, -2, 2, -1, 1, 0]
+STEPS = [0, -1, 1, -2, 2, -3, 3, 4]
+LANES = [0, -1, 1, -2]
 DEEP = NZ // 2
 KEYS = NX * TOK
+
+
+def around(s):
+    return [s] if s in (0, DEEP) else [-s, s]
+
+
+def opposite(step):
+    return step if step == DEEP else -step
 
 
 def layer_kernel(
@@ -234,7 +247,7 @@
     q_ref, do_ref, gate_ref, up_ref, down_ref,
     send, recv, rows_ref, part, pmate, ysend, yrecv, full,
     kv, qs, dos, e_ref, mj, m_ref, l_ref, o_ref, d_ref, dq_acc,
-    dkv, dmate, zsend, zrecv, own4, xsend, xrecv, tsend, trecv, kg, back,
+    dkv, dmate, zsend, zrecv, sums, xsend, xrecv, tsend, trecv, kg, back,
     s_in, s_l, s_far, r_far, s_kx, r_kx, s_kz, r_kz, s_km, r_km,
     s_pm, r_pm, s_y, r_y, s_g, r_g, s_gm, r_gm,
     s_dm, r_dm, s_z, r_z, s_x, r_x, s_t, r_t, s_c, r_c, s_cm, r_cm, s_ret, r_ret,
@@ -280,75 +293,129 @@
     pl.semaphore_wait(barrier, len(near) + NE - 1)
 
     sends = []
+    core_sends = ([], [])
 
     def go(c):
         c.start()
         sends.append(c)
 
+    def by_core(zero, one):
+        for core, f in enumerate((zero, one)):
+
+            def start(make, *args, core=core):
+                make(*args).start()
+                core_sends[core].append((make, args))
+
+            @pl.when(k == core)
+            def _(f=f, start=start):
+                f(start)
+
     begin, finish = exchange(here, send, recv, s_far, r_far)
-    begin(1, NE)
     local = pltpu.make_async_copy(send.at[e], recv.at[e], s_l.at[1])
     local.start()
 
-    def block(step):
-        return kv.at[k, z, here.at_x(step)]
-
-    def slab(step):
-        return kv.at[k, here.at_z(step)]
-
-    def xcopy(i, origin, to):
-        return remote(block(origin), block(origin), s_kx.at[i], r_kx.at[i], here.dev_x(to))
-
-    def zcopy(i, origin, to):
-        return remote(slab(origin), slab(origin), s_kz.at[i], r_kz.at[i], here.dev_z(to))
-
-    def kv_mate(i, origin):
-        return remote(slab(origin), slab(origin), s_km.at[i], r_km.at[i], here.mate)
-
-    go(xcopy(0, 0, 1))
-    go(xcopy(2, 0, -1))
-    xcopy(0, -1, 1).wait_recv()
-    go(xcopy(1, -1, 1))
-    xcopy(2, 1, -1).wait_recv()
-    xcopy(1, -2, 1).wait_recv()
-    go(zcopy(0, 0, 1))
-    go(zcopy(DEEP, 0, -1))
-    go(kv_mate(0, 0))
-
-    def kv_step(s):
-        zcopy(s - 1, -s, 1).wait_recv()
-        if s < DEEP:
-            go(zcopy(s, -s, 1))
-        go(kv_mate(s, -s))
-        if s < DEEP:
-            zcopy(DEEP + s - 1, s, -1).wait_recv()
-            if s < DEEP - 1:
-                go(zcopy(DEEP + s, s, -1))
-            go(kv_mate(DEEP + s, s))
-
-    def kv_from_mate(i, step):
-        spot = kv.at[1 - k, here.at_z(step)]
-        remote(spot, spot, s_km.at[i], r_km.at[i], here.mate).wait_recv()
-
-    def kv_ready(d):
-        kv_from_mate(d, d)
-        if 0 < d < DEEP:
-            kv_from_mate(DEEP + d, -d)
-
-    for c in loads:
-        c.wait()
-    local.wait()
-    finish()
-
-    table = pack_table(False)
-    n = 4 * PACK
-    for g in range(NE // 8):
-        slabs = recv[g * 8 : (g + 1) * 8].reshape(n, 128)
-        packed = dot(table, slabs).astype(BF16)
-        for i in range(4):
-            rows_ref[i // 2, g * PACK : (g + 1) * PACK, (i % 2) * 128 : (i % 2 + 1) * 128] = packed[
-                i * PACK : (i + 1) * PACK, :
-            ]
+    def kz(j, zs, xs, to):
+        spot = kv.at[k, here.at_z(zs), here.at_x(xs)]
+        return remote(spot, spot, s_kz.at[j], r_kz.at[j], here.dev_z(to))
+
+    def kx(j, zs, xs, to):
+        spot = kv.at[k, here.at_z(zs), here.at_x(xs)]
+        return remote(spot, spot, s_kx.at[j], r_kx.at[j], here.dev_x(to))
+
+    def kv_mate(step):
+        i, spot = STEPS.index(step), kv.at[k, here.at_z(step)]
+        return remote(spot, spot, s_km.at[i], r_km.at[i], here.mate)
+
+    def lane_start(start, xs):
+        i = LANES.index(xs) * 8
+        start(kz, i, 0, xs, 1)
+        start(kz, i + DEEP, 0, xs, -1)
+
+    def lane_step(start, s):
+        for i, xs in enumerate(LANES):
+            kz(i * 8 + s - 1, -s, xs, 1).wait_recv()
+            if s < DEEP:
+                start(kz, i * 8 + s, -s, xs, 1)
+                kz(i * 8 + DEEP + s - 1, s, xs, -1).wait_recv()
+                if s < DEEP - 1:
+                    start(kz, i * 8 + DEEP + s, s, xs, -1)
+        for step in around(s):
+            start(kv_mate, step)
+
+    def cross_start(start, s):
+        for step in around(s):
+            i = STEPS.index(step) * 3
+            start(kx, i, step, 0, 1)
+            start(kx, i + 2, step, 0, -1)
+
+    def cross_mid(start, s):
+        for step in around(s):
+            i = STEPS.index(step) * 3
+            kx(i, step, -1, 1).wait_recv()
+            start(kx, i + 1, step, -1, 1)
+            kx(i + 2, step, 1, -1).wait_recv()
+
+    def cross_end(start, s):
+        for step in around(s):
+            kx(STEPS.index(step) * 3 + 1, step, -2, 1).wait_recv()
+            start(kv_mate, step)
+
+    def kv_step(t):
+        def zero(start):
+            if t == 0:
+                start(kx, 0, 0, 0, 1)
+                start(kx, 2, 0, 0, -1)
+                lane_start(start, 0)
+            elif t == 1:
+                kx(0, 0, -1, 1).wait_recv()
+                start(kx, 1, 0, -1, 1)
+                lane_start(start, -1)
+                kx(2, 0, 1, -1).wait_recv()
+                lane_start(start, 1)
+            elif t == 2:
+                kx(1, 0, -2, 1).wait_recv()
+                lane_start(start, -2)
+                start(kv_mate, 0)
+            else:
+                lane_step(start, t - 2)
+
+        def one(start):
+            if t == 0:
+                start(kz, 0, 0, 0, 1)
+                start(kz, DEEP, 0, 0, -1)
+                cross_start(start, 0)
+                return
+            if t <= DEEP:
+                kz(t - 1, -t, 0, 1).wait_recv()
+                if t < DEEP:
+                    start(kz, t, -t, 0, 1)
+                    kz(DEEP + t - 1, t, 0, -1).wait_recv()
+                    if t < DEEP - 1:
+                        start(kz, DEEP + t, t, 0, -1)
+                cross_start(start, t)
+            if t <= DEEP + 1:
+                cross_mid(start, t - 1)
+            if t >= 2:
+                cross_end(start, t - 2)
+
+        by_core(zero, one)
+
+    def kv_ready(s):
+        for step in around(s):
+            i, spot = STEPS.index(opposite(step)), kv.at[1 - k, here.at_z(step)]
+            remote(spot, spot, s_km.at[i], r_km.at[i], here.mate).wait_recv()
+
+    def pack():
+        table = pack_table(False, PACK)
+        for g in range(NE // 8):
+            slabs = [recv[source(y, i)] for y in (2 * g, 2 * g + 1) for i in range(NX)]
+            packed = dot(table, jnp.concatenate(slabs, axis=0)).astype(BF16)
+            for i in range(4):
+                lanes = slice((i % 2) * 128, (i % 2 + 1) * 128)
+                rows_ref[i // 2, g * PACK : (g + 1) * PACK, lanes] = packed[
+                    i * PACK : (i + 1) * PACK, :
+                ]
+
     first = first_local(ROWS)
 
     def product(m):
@@ -440,10 +507,10 @@
                     go(gcopy(DEEP + s, m, s, -1))
                 go(g_mate(DEEP + s, m, s))
 
-    def gather_from_mate():
+    def gather_ready(s):
         for m in range(3):
-            pairs = [(s, s) for s in range(DEEP + 1)] + [(DEEP + s, -s) for s in range(1, DEEP)]
-            for i, step in pairs:
+            for step in around(s):
+                i = s if step != -s or s == 0 else DEEP + s
                 spot = full.at[1 - k, here.at_y(step), m]
                 j = m * 8 + i
                 remote(spot, spot, s_gm.at[j], r_gm.at[j], here.mate).wait_recv()
@@ -497,7 +564,7 @@
         dkv[0, j] = (dot(ds, qs[...]) * SCALE).astype(BF16).reshape(NX, TOK, HEAD)
         dkv[1, j] = dot(p.astype(BF16), dos[...]).astype(BF16).reshape(NX, TOK, HEAD)
         dq_acc[...] += t_dot(keys, ds)
-        i = ORDER.index(step if step == DEEP else -step)
+        i = ORDER.index(opposite(step))
         go(remote(dkv.at[1 - k, j], dmate.at[j], s_dm.at[i], r_dm.at[i], here.mate))
 
     def query_grad():
@@ -505,57 +572,111 @@
         for h in range(heads):
             dq_ref[:, h * HEAD : (h + 1) * HEAD] = turned[h * TOK : (h + 1) * TOK, :].astype(BF16)
 
-    def dkv_in(i):
-        d = here.at_z(ORDER[i])
+    def dkv_in(step):
+        i, d = ORDER.index(step), here.at_z(step)
         remote(dkv.at[k, d], dmate.at[d], s_dm.at[i], r_dm.at[i], here.mate).wait_recv()
         return d
 
-    def zslot(i, to):
-        return remote(zsend.at[i], zrecv.at[i], s_z.at[i], r_z.at[i], here.dev_z(to))
-
-    def z_step(s):
-        d = dkv_in(ORDER.index(DEEP - s))
-        if s == 0:
-            zsend[0] = add16(dkv[k, d], dmate[d]).astype(BF16)
-        else:
-            zslot(s - 1, 1).wait_recv()
-            zsend[s] = add16(dkv[k, d], dmate[d], zrecv[s - 1]).astype(BF16)
-        go(zslot(s, 1))
-        if s < DEEP - 1:
-            d = dkv_in(ORDER.index(s + 1 - DEEP))
-            i = DEEP + s
-            if s == 0:
-                zsend[i] = add16(dkv[k, d], dmate[d]).astype(BF16)
-            else:
-                zslot(i - 1, -1).wait_recv()
-                zsend[i] = add16(dkv[k, d], dmate[d], zrecv[i - 1]).astype(BF16)
-            go(zslot(i, -1))
+    def zslot(i, n, to):
+        spot = pl.ds(i * n, n)
+        return remote(zsend.at[spot], zrecv.at[spot], s_z.at[i], r_z.at[i], here.dev_z(to))
 
     def xslot(i, to):
         return remote(xsend.at[i], xrecv.at[i], s_x.at[i], r_x.at[i], here.dev_x(to))
 
-    def x_first():
-        d = dkv_in(ORDER.index(0))
-        zslot(2 * DEEP - 2, -1).wait_recv()
-        zslot(DEEP - 1, 1).wait_recv()
-        own4[...] = add16(dkv[k, d], dmate[d], zrecv[2 * DEEP - 2], zrecv[DEEP - 1])
-        xsend[0] = own4[here.at_x(2)].astype(BF16)
-        go(xslot(0, 1))
-        xsend[2] = own4[here.at_x(-1)].astype(BF16)
-        go(xslot(2, -1))
-
-    def x_second():
-        xslot(0, 1).wait_recv()
-        xsend[1] = add16(own4[here.at_x(1)], xrecv[0]).astype(BF16)
-        go(xslot(1, 1))
+    def wide_step(start, s, to):
+        d = dkv_in(DEEP - s if to > 0 else s + 1 - DEEP)
+        for h in range(2):
+            i = (s if to > 0 else DEEP + s) * 2 + h
+            blocks = pl.ds(2 * h, 2)
+            terms = [dkv[k, d, blocks], dmate[d, blocks]]
+            if s:
+                zslot(i - 2, 2, to).wait_recv()
+                terms.append(zrecv[2 * i - 4 : 2 * i - 2])
+            zsend[2 * i : 2 * i + 2] = add16(*terms).astype(BF16)
+            start(zslot, i, 2, to)
+
+    def thin_step(start, s, to):
+        i = s if to > 0 else DEEP + s
+        total = sums[STEPS.index(DEEP - s if to > 0 else s + 1 - DEEP)]
+        if s:
+            zslot(i - 1, 1, to).wait_recv()
+            total = total + zrecv[i - 1].astype(F32)
+        zsend[i] = total.astype(BF16)
+        start(zslot, i, 1, to)
+
+    def x_start(start, s):
+        for step in around(s):
+            d, i = dkv_in(step), STEPS.index(step) * 3
+            for slot, xs in ((0, 2), (2, -1)):
+                j = here.at_x(xs)
+                xsend[i + slot] = add16(dkv[k, d, j], dmate[d, j]).astype(BF16)
+            start(xslot, i, 1)
+            start(xslot, i + 2, -1)
+
+    def x_mid(start, s):
+        for step in around(s):
+            d, i = here.at_z(step), STEPS.index(step) * 3
+            j = here.at_x(1)
+            xslot(i, 1).wait_recv()
+            xsend[i + 1] = add16(dkv[k, d, j], dmate[d, j], xrecv[i]).astype(BF16)
+            start(xslot, i + 1, 1)
+
+    def x_end(s):
+        for step in around(s):
+            d, i = here.at_z(step), STEPS.index(step) * 3
+            xslot(i + 2, -1).wait_recv()
+            xslot(i + 1, 1).wait_recv()
+            sums[i // 3] = add16(dkv[k, d, x], dmate[d, x], xrecv[i + 1], xrecv[i + 2])
+
+    def grad_step(t):
+        def zero(start):
+            if t < DEEP:
+                if t:
+                    wide_step(start, t - 1, -1)
+                wide_step(start, t, 1)
+            elif t == DEEP:
+                d = dkv_in(0)
+                for i in (3, 2 * DEEP - 2):
+                    for h in range(2):
+                        zslot(2 * i + h, 2, 1 if i == 3 else -1).wait_recv()
+                last = pl.ds(4 * (2 * DEEP - 2), 4)
+                sums[0:4] = add16(dkv[k, d], dmate[d], zrecv[12:16], zrecv[last])
+                xsend[0] = sums[here.at_x(2)].astype(BF16)
+                start(xslot, 0, 1)
+                xsend[2] = sums[here.at_x(-1)].astype(BF16)
+                start(xslot, 2, -1)
+            elif t == DEEP + 1:
+                xslot(0, 1).wait_recv()
+                xsend[1] = (sums[here.at_x(1)] + xrecv[0].astype(F32)).astype(BF16)
+                start(xslot, 1, 1)
+            else:
+                xslot(2, -1).wait_recv()
+                xslot(1, 1).wait_recv()
+                tsend[...] = (sums[x] + add16(xrecv[2], xrecv[1])).astype(BF16)
+
+        def one(start):
+            if t <= DEEP:
+                x_start(start, DEEP - t)
+            if 1 <= t <= DEEP + 1:
+                x_mid(start, DEEP + 1 - t)
+            if t >= 2:
+                x_end(DEEP + 2 - t)
+                if t < DEEP + 2:
+                    thin_step(start, t - 2, 1)
+                    if t > 2:
+                        thin_step(start, t - 3, -1)
+                else:
+                    zslot(DEEP - 1, 1, 1).wait_recv()
+                    zslot(2 * DEEP - 2, 1, -1).wait_recv()
+                    total = sums[0] + add16(zrecv[DEEP - 1], zrecv[2 * DEEP - 2])
+                    tsend[...] = total.astype(BF16)
+
+        by_core(zero, one)
+        if t == DEEP + 2:
+            go(twin)
 
     twin = remote(tsend, trecv, s_t.at[0], r_t.at[0], here.twin)
-
-    def x_third():
-        xslot(2, -1).wait_recv()
-        xslot(1, 1).wait_recv()
-        tsend[...] = add16(own4[x], xrecv[2], xrecv[1]).astype(BF16)
-        go(twin)
 
     def spot(which, step):
         head = here.at_y(step) // 2
@@ -581,86 +702,127 @@
         remote(kg, spot(1 - k, 0), s_cm.at[3], r_cm.at[3], here.mate).wait_recv()
         mine.wait()
 
-    ret_begin, ret_finish = exchange(here, back, ret_ref, s_ret, r_ret)
+    ret_one, ret_finish = exchange(here, back, ret_ref, s_ret, r_ret, True)
     ret_local = pltpu.make_async_copy(back.at[e], ret_ref.at[e], s_l.at[3])
 
-    def experts_out():
+    def experts_out(s):
+        blocks = [here.at_y(step) for step in around(s)]
+        rows = len(blocks) * YROWS
+        near = first_local(rows)
+
         def both(m, weight, transposed):
-            halves = [full[c, :, m].reshape(ROWS, HALF) for c in range(2)]
-            whole = jnp.concatenate(halves, axis=1)
+            parts = [
+                jnp.concatenate([full[0, y, m], full[1, y, m]], axis=1) for y in blocks
+            ]
+            whole = jnp.concatenate(parts, axis=0)
             f = dot_t if transposed else dot
-            return jnp.where(first, f(whole, weight[0]), f(whole, weight[1]))
+            return jnp.where(near, f(whole, weight[0]), f(whole, weight[1]))
 
         route_out = both(0, down_ref, False).astype(BF16)
         route_in = (both(1, gate_ref, True) + both(2, up_ref, True)).astype(BF16)
         quarters = [route_out[:, :128], route_out[:, 128:], route_in[:, :128], route_in[:, 128:]]
-        unpack = pack_table(True)
-        for g in range(NE // 8):
-            stacked = jnp.concatenate([q[g * PACK : (g + 1) * PACK] for q in quarters], axis=0)
-            back[g * 8 : (g + 1) * 8] = dot(unpack, stacked).astype(BF16).reshape(8, SLAB, 128)
-        ret_begin(1, NE)
-        ret_local.start()
-
+        out = dot(pack_table(True, rows), jnp.concatenate(quarters, axis=0)).astype(BF16)
+        for b, y in enumerate(blocks):
+            for i in range(NX):
+                dest = source(y, i)
+                r = (b * NX + i) * SLAB
+                back[dest] = out[r : r + SLAB]
+                offset = (dest + NE - e) % NE
+
+                @pl.when(offset != 0)
+                def _():
+                    ret_one(offset).start()
+
+                @pl.when(offset == 0)
+                def _():
+                    ret_local.start()
+
+    kv_step(0)
+    begin(1, 9)
+    kv_step(1)
+    begin(9, 17)
+    kv_step(2)
+    begin(17, 25)
+    for c in loads:
+        c.wait()
+    stack()
+    kv_step(3)
+    begin(25, NE)
+    kv_ready(0)
+    forward(0)
+    kv_step(4)
+    kv_ready(1)
+    forward(-1)
+    forward(1)
+    local.wait()
+    finish()
+    pack()
     product(0)
-    kv_step(1)
+    kv_step(5)
     product(1)
     y_step(0, 0)
     product(2)
     y_step(0, 1)
-    kv_step(2)
+    kv_step(6)
     y_step(0, 2)
-    stack()
-    kv_ready(0)
-    forward(0)
-    for m in range(3):
-        y_step(1, m)
-    kv_step(3)
-    kv_ready(1)
-    forward(-1)
-    forward(1)
-    for m in range(3):
-        y_step(2, m)
-    kv_step(4)
     kv_ready(2)
     forward(-2)
     forward(2)
     for m in range(3):
-        y_step(3, m)
+        y_step(1, m)
     kv_ready(3)
     forward(-3)
     forward(3)
-    activate()
+    for m in range(3):
+        y_step(2, m)
     kv_ready(4)
     forward(4)
     normalize()
+    for m in range(3):
+        y_step(3, m)
+    backward(4)
+    grad_step(0)
+    backward(-3)
+    activate()
+    backward(3)
+    grad_step(1)
     gather_step(1)
-    backward(4)
-    backward(-3)
+    gather_ready(0)
+    experts_out(0)
+    backward(-2)
+    backward(2)
+    grad_step(2)
     gather_step(2)
-    backward(3)
-    z_step(0)
-    backward(-2)
+    gather_ready(1)
+    experts_out(1)
+    backward(-1)
+    backward(1)
+    grad_step(3)
     gather_step(3)
-    backward(2)
-    z_step(1)
-    backward(-1)
+    gather_ready(2)
+    experts_out(2)
+    backward(0)
+    grad_step(4)
     gather_step(4)
-    gather_from_mate()
-    experts_out()
-    backward(1)
-    z_step(2)
-    backward(0)
-    z_step(3)
+    gather_ready(3)
+    experts_out(3)
+    grad_step(5)
+    gather_ready(4)
+    experts_out(4)
     query_grad()
-    x_first()
-    x_second()
-    x_third()
+    grad_step(6)
     spread()
     spread_end()
     ret_finish()
     ret_local.wait()
     for c in sends:
         c.wait_send()
+    for core in range(2):
+
+        @pl.when(k == core)
+        def _(core=core):
+            for make, args in core_sends[core]:
+                make(*args).wait_send()
 
 
 def vmem():
@@ -703,8 +865,8 @@
     def b16(*dims):
         return pltpu.VMEM(dims, BF16)
 
-    sems = [5, 4, NE, NE, 3, 3, 8, 8, 8, 8, 24, 24, 21, 21, 21, 21, 24, 24]
-    sems += [8, 8, 7, 7, 3, 3, 1, 1, 3, 3, 4, 4, NE, NE]
+    sems = [5, 4, NE, NE, 24, 24, 32, 32, 8, 8, 24, 24, 21, 21, 21, 21, 24, 24]
+    sems += [8, 8, 14, 14, 24, 24, 1, 1, 3, 3, 4, 4, NE, NE]
     attn_out, dq, returned, kvg = call(
         layer_kernel,
         (shape(*q.shape), shape(*q.shape), shape(NE, SLAB, 128), shape(2, TOK, 4 * HEAD)),
@@ -716,8 +878,8 @@
             b16(2, NZ, *zslab), b16(width, HEAD), b16(width, HEAD), b16(NZ, KEYS, width),
             f32(NZ, 1, width), f32(1, width), f32(1, width), f32(HEAD, width), f32(1, width),
             f32(HEAD, width),
-            b16(2, NZ, *zslab), b16(NZ, *zslab), b16(7, *zslab), b16(7, *zslab), f32(*zslab),
-            b16(3, *block), b16(3, *block), b16(*block), b16(*block), b16(*block),
+            b16(2, NZ, *zslab), b16(NZ, *zslab), b16(28, *block), b16(28, *block), f32(8, *block),
+            b16(24, *block), b16(24, *block), b16(*block), b16(*block), b16(*block),
             b16(NE, SLAB, 128),
         ]
         + [dma(n) for n in sems],

time: 110 us -> 101 us (0.918)
  Pallas kernels: 109 us -> 100 us
    pallas_call x2, Pallas kernels: 109 us -> 100 us  [call(): pl.pallas_call(kernel, out_shape=outs, in_specs=specs or [vmem()] * len(a...]
where the time goes in v3:
time: 101 us
  Pallas kernels  100 us (99%)
    pallas_call x2, Pallas kernels, call(): pl.pallas_call(kernel, out_shape=outs, in_specs=specs or [vmem()] * len(a...  100 us

profile of v3, /device:TPU:1, one launch (start us, length us, event | category | flops | bytes accessed | tf_op | source)
XLA Modules:
  0.0 100.9 jit_solution(18272905078102083357)
XLA Ops:
  0.6 97.0 %layer.1 = (bf16[128,512]{1,0:T(8,128)(2,1)}, bf16[128,512]{1,0:T(8,128)(2,1)}, bf16[32,48,128]{2,1,0:T(8,128)(2,1)}, bf16[2,128,512]{2,1,0:T(8,128)(2,1)}) custom-call(s32[2,128]{1,0:T(2,128)} %bitcast.4, f32[2,128]{1,0:T(2,128)} %bitcast.6, bf16[128,256]{1,0:T(8,128)(2,1)} %x_ref.1, bf16[128,256]{1,0:T(8,128)(2,1)} %g_ref.1, bf16[128,512]{1,0:T(8,128)(2,1)} %key_ref.1, ...), custom_call_target="tpu_custom_call" | custom-call | tf_op jit(solution)/shard_map/layer/pallas_call | solution.py:840
  97.7 3.2 %combine.1 = (bf16[128,256]{1,0:T(8,128)(2,1)}, bf16[128,256]{1,0:T(8,128)(2,1)}, bf16[128,512]{1,0:T(8,128)(2,1)}, bf16[128,512]{1,0:T(8,128)(2,1)}, bf16[128,5...) custom-call(s32[2,128]{1,0:T(2,128)} %bitcast.5, f32[2,128]{1,0:T(2,128)} %bitcast.7, bf16[1536,128]{1,0:T(8,128)(2,1)} %bitcast.3, ...), custom_call_target="tpu_custom_call" | custom-call | tf_op jit(solution)/shard_map/combine/pallas_call | solution.py:840

commit v4 on v3

--- a/solution.py
+++ b/solution.py
@@ -186,37 +186,35 @@
     )
 
 
+def remote(src, dst, send, recv, device):
+    return pltpu.make_async_remote_copy(
+        src_ref=src, dst_ref=dst, send_sem=send, recv_sem=recv, device_id=device,
+        device_id_type=MESH,
+    )
+
+
 def exchange(here, send_ref, recv_ref, send_sem, recv_sem, single=False):
-    def desc(o):
+    def one(o):
         dest = (here.e + o) % NE
         return remote(
-            send_ref.at[dest], recv_ref.at[here.e], send_sem.at[o], recv_sem.at[o],
+            send_ref.at[dest], recv_ref.at[here.e], send_sem.at[0], recv_sem.at[0],
             {"exp": dest, "ctx": here.c},
         )
 
-    def incoming(o):
-        source = (here.e + NE - o) % NE
-        return remote(
-            send_ref.at[source], recv_ref.at[source], send_sem.at[o], recv_sem.at[o],
-            {"exp": source, "ctx": here.c},
-        )
-
     def begin(first, last):
         def go(o, carry):
-            desc(o).start()
+            one(o).start()
             return carry
 
         lax.fori_loop(first, last, go, 0)
 
     def finish():
-        def go(o, carry):
-            desc(o).wait_send()
-            incoming(o).wait_recv()
-            return carry
-
-        lax.fori_loop(1, NE, go, 0)
-
-    return (desc if single else begin), finish
+        rest = pl.ds(0, NE - 1)
+        every = remote(send_ref.at[rest], recv_ref.at[rest], send_sem.at[0], recv_sem.at[0], here.mate)
+        every.wait_send()
+        every.wait_recv()
+
+    return one, begin, finish
 
 
 def add16(*refs):
@@ -293,7 +291,6 @@
     pl.semaphore_wait(barrier, len(near) + NE - 1)
 
     sends = []
-    core_sends = ([], [])
 
     def go(c):
         c.start()
@@ -302,29 +299,28 @@
     def by_core(zero, one):
         for core, f in enumerate((zero, one)):
 
-            def start(make, *args, core=core):
+            def start(make, *args):
                 make(*args).start()
-                core_sends[core].append((make, args))
 
             @pl.when(k == core)
             def _(f=f, start=start):
                 f(start)
 
-    begin, finish = exchange(here, send, recv, s_far, r_far)
+    far_one, begin, finish = exchange(here, send, recv, s_far, r_far)
     local = pltpu.make_async_copy(send.at[e], recv.at[e], s_l.at[1])
     local.start()
 
     def kz(j, zs, xs, to):
         spot = kv.at[k, here.at_z(zs), here.at_x(xs)]
-        return remote(spot, spot, s_kz.at[j], r_kz.at[j], here.dev_z(to))
+        return remote(spot, spot, s_kz.at[0], r_kz.at[j], here.dev_z(to))
 
     def kx(j, zs, xs, to):
         spot = kv.at[k, here.at_z(zs), here.at_x(xs)]
-        return remote(spot, spot, s_kx.at[j], r_kx.at[j], here.dev_x(to))
+        return remote(spot, spot, s_kx.at[0], r_kx.at[j], here.dev_x(to))
 
     def kv_mate(step):
         i, spot = STEPS.index(step), kv.at[k, here.at_z(step)]
-        return remote(spot, spot, s_km.at[i], r_km.at[i], here.mate)
+        return remote(spot, spot, s_km.at[0], r_km.at[i], here.mate)
 
     def lane_start(start, xs):
         i = LANES.index(xs) * 8
@@ -403,7 +399,7 @@
     def kv_ready(s):
         for step in around(s):
             i, spot = STEPS.index(opposite(step)), kv.at[1 - k, here.at_z(step)]
-            remote(spot, spot, s_km.at[i], r_km.at[i], here.mate).wait_recv()
+            remote(spot, spot, s_km.at[0], r_km.at[i], here.mate).wait_recv()
 
     def pack():
         table = pack_table(False, PACK)
@@ -430,54 +426,49 @@
         for c in range(2):
             for y in range(NY):
                 part[c, y, m] = whole[y * YROWS : (y + 1) * YROWS, c * HALF : (c + 1) * HALF]
-        for i, step in enumerate(ORDER):
-            d = here.at_y(-step)
-            j = m * 8 + i
-            go(remote(part.at[1 - k, d, m], pmate.at[d, m], s_pm.at[j], r_pm.at[j], here.mate))
-
-    def part_in(i, m):
-        d = here.at_y(ORDER[i])
-        j = m * 8 + i
-        remote(part.at[k, d, m], pmate.at[d, m], s_pm.at[j], r_pm.at[j], here.mate).wait_recv()
-        return d
+        go(part_mate(m))
+
+    def part_mate(m):
+        return remote(part.at[1 - k, :, m], pmate.at[:, m], s_pm.at[m], r_pm.at[m], here.mate)
 
     def yslot(i, m, to):
         j = m * 7 + i
-        return remote(ysend.at[j], yrecv.at[j], s_y.at[j], r_y.at[j], here.dev_y(to))
+        return remote(ysend.at[j], yrecv.at[j], s_y.at[0], r_y.at[j], here.dev_y(to))
 
     def y_step(s, m):
-        d = part_in(ORDER.index(DEEP - s), m)
+        d = here.at_y(DEEP - s)
+        if s == 0:
+            part_mate(m).wait_recv()
         j = m * 7 + s
         if s == 0:
             ysend[j] = add16(part[k, d, m], pmate[d, m]).astype(BF16)
         else:
             yslot(s - 1, m, 1).wait_recv()
             ysend[j] = add16(part[k, d, m], pmate[d, m], yrecv[j - 1]).astype(BF16)
-        go(yslot(s, m, 1))
+        yslot(s, m, 1).start()
         if s < DEEP - 1:
-            d = part_in(ORDER.index(s + 1 - DEEP), m)
+            d = here.at_y(s + 1 - DEEP)
             j = m * 7 + DEEP + s
             if s == 0:
                 ysend[j] = add16(part[k, d, m], pmate[d, m]).astype(BF16)
             else:
                 yslot(DEEP + s - 1, m, -1).wait_recv()
                 ysend[j] = add16(part[k, d, m], pmate[d, m], yrecv[j - 1]).astype(BF16)
-            go(yslot(DEEP + s, m, -1))
+            yslot(DEEP + s, m, -1).start()
 
     def gcopy(i, m, origin, to):
         spot = full.at[k, here.at_y(origin), m]
         j = m * 7 + i
-        return remote(spot, spot, s_g.at[j], r_g.at[j], here.dev_y(to))
-
-    def g_mate(i, m, origin):
-        spot = full.at[k, here.at_y(origin), m]
-        j = m * 8 + i
-        return remote(spot, spot, s_gm.at[j], r_gm.at[j], here.mate)
+        return remote(spot, spot, s_g.at[0], r_g.at[j], here.dev_y(to))
+
+    def g_mate(i, origin):
+        spot = full.at[k, here.at_y(origin)]
+        return remote(spot, spot, s_gm.at[0], r_gm.at[i], here.mate)
 
     def activate():
         total = []
         for m in range(3):
-            d = part_in(ORDER.index(0), m)
+            d = here.y
             yslot(2 * DEEP - 2, m, -1).wait_recv()
             yslot(DEEP - 1, m, 1).wait_recv()
             total.append(
@@ -490,30 +481,27 @@
         full[k, here.y, 1] = (hidden_grad * up * sig * (1.0 + gate * (1.0 - sig))).astype(BF16)
         full[k, here.y, 2] = (hidden_grad * act).astype(BF16)
         for m in range(3):
-            go(gcopy(0, m, 0, 1))
-            go(gcopy(DEEP, m, 0, -1))
-        for m in range(3):
-            go(g_mate(0, m, 0))
+            gcopy(0, m, 0, 1).start()
+            gcopy(DEEP, m, 0, -1).start()
+        g_mate(0, 0).start()
 
     def gather_step(s):
         for m in range(3):
             gcopy(s - 1, m, -s, 1).wait_recv()
             if s < DEEP:
-                go(gcopy(s, m, -s, 1))
-            go(g_mate(s, m, -s))
-            if s < DEEP:
+                gcopy(s, m, -s, 1).start()
                 gcopy(DEEP + s - 1, m, s, -1).wait_recv()
                 if s < DEEP - 1:
-                    go(gcopy(DEEP + s, m, s, -1))
-                go(g_mate(DEEP + s, m, s))
+                    gcopy(DEEP + s, m, s, -1).start()
+        g_mate(s, -s).start()
+        if s < DEEP:
+            g_mate(DEEP + s, s).start()
 
     def gather_ready(s):
-        for m in range(3):
-            for step in around(s):
-                i = s if step != -s or s == 0 else DEEP + s
-                spot = full.at[1 - k, here.at_y(step), m]
-                j = m * 8 + i
-                remote(spot, spot, s_gm.at[j], r_gm.at[j], here.mate).wait_recv()
+        for step in around(s):
+            i = s if step != -s or s == 0 else DEEP + s
+            spot = full.at[1 - k, here.at_y(step)]
+            remote(spot, spot, s_gm.at[0], r_gm.at[i], here.mate).wait_recv()
 
     heads = q_ref.shape[1] // HEAD
     width = heads * TOK
@@ -565,7 +553,7 @@
         dkv[1, j] = dot(p.astype(BF16), dos[...]).astype(BF16).reshape(NX, TOK, HEAD)
         dq_acc[...] += t_dot(keys, ds)
         i = ORDER.index(opposite(step))
-        go(remote(dkv.at[1 - k, j], dmate.at[j], s_dm.at[i], r_dm.at[i], here.mate))
+        remote(dkv.at[1 - k, j], dmate.at[j], s_dm.at[0], r_dm.at[i], here.mate).start()
 
     def query_grad():
         turned = (dq_acc[...] * SCALE).T
@@ -574,15 +562,15 @@
 
     def dkv_in(step):
         i, d = ORDER.index(step), here.at_z(step)
-        remote(dkv.at[k, d], dmate.at[d], s_dm.at[i], r_dm.at[i], here.mate).wait_recv()
+        remote(dkv.at[k, d], dmate.at[d], s_dm.at[0], r_dm.at[i], here.mate).wait_recv()
         return d
 
     def zslot(i, n, to):
         spot = pl.ds(i * n, n)
-        return remote(zsend.at[spot], zrecv.at[spot], s_z.at[i], r_z.at[i], here.dev_z(to))
+        return remote(zsend.at[spot], zrecv.at[spot], s_z.at[0], r_z.at[i], here.dev_z(to))
 
     def xslot(i, to):
-        return remote(xsend.at[i], xrecv.at[i], s_x.at[i], r_x.at[i], here.dev_x(to))
+        return remote(xsend.at[i], xrecv.at[i], s_x.at[0], r_x.at[i], here.dev_x(to))
 
     def wide_step(start, s, to):
         d = dkv_in(DEEP - s if to > 0 else s + 1 - DEEP)
@@ -687,22 +675,24 @@
     def spread():
         twin.wait_recv()
         kg[...] = add16(tsend[...], trecv[...]).astype(BF16)
-        for i, step in enumerate((2, 4, 6)):
+        for i, step in enumerate((4, 2, 6)):
             go(remote(kg, spot(k, 0), s_c.at[i], r_c.at[i], here.dev_y(step)))
         go(remote(kg, spot(k, 0), s_cm.at[3], r_cm.at[3], here.mate))
         mine.start()
 
     def spread_end():
-        for i, step in enumerate((2, 4, 6)):
-            remote(kg, spot(k, -step), s_c.at[i], r_c.at[i], here.dev_y(-step)).wait_recv()
-            go(remote(spot(k, -step), spot(k, -step), s_cm.at[i], r_cm.at[i], here.mate))
-        for i, step in enumerate((2, 4, 6)):
-            there = spot(1 - k, step)
+        order = (4, 2, 6)
+        for i in (1, 2, 0):
+            there = spot(k, -order[i])
+            remote(kg, there, s_c.at[i], r_c.at[i], here.dev_y(-order[i])).wait_recv()
+            go(remote(there, there, s_cm.at[i], r_cm.at[i], here.mate))
+        remote(kg, spot(1 - k, 0), s_cm.at[3], r_cm.at[3], here.mate).wait_recv()
+        for i in (1, 2, 0):
+            there = spot(1 - k, order[i])
             remote(there, there, s_cm.at[i], r_cm.at[i], here.mate).wait_recv()
-        remote(kg, spot(1 - k, 0), s_cm.at[3], r_cm.at[3], here.mate).wait_recv()
         mine.wait()
 
-    ret_one, ret_finish = exchange(here, back, ret_ref, s_ret, r_ret, True)
+    ret_one, ret_begin, ret_finish = exchange(here, back, ret_ref, s_ret, r_ret)
     ret_local = pltpu.make_async_copy(back.at[e], ret_ref.at[e], s_l.at[3])
 
     def experts_out(s):
@@ -737,92 +727,107 @@
                 def _():
                     ret_local.start()
 
+    def each_y(s):
+        for m in range(3):
+            y_step(s, m)
+
+    def drain(sem, ref):
+        remote(ref, ref, sem.at[0], sem.at[0], here.mate).wait_send()
+
     kv_step(0)
-    begin(1, 9)
+    begin(1, 17)
     kv_step(1)
-    begin(9, 17)
-    kv_step(2)
-    begin(17, 25)
+    begin(17, NE)
     for c in loads:
         c.wait()
     stack()
+    kv_step(2)
     kv_step(3)
-    begin(25, NE)
-    kv_ready(0)
-    forward(0)
-    kv_step(4)
-    kv_ready(1)
-    forward(-1)
-    forward(1)
     local.wait()
     finish()
     pack()
     product(0)
-    kv_step(5)
+    kv_step(4)
     product(1)
     y_step(0, 0)
     product(2)
     y_step(0, 1)
+    kv_step(5)
+    y_step(0, 2)
+    kv_ready(0)
+    forward(0)
+    kv_ready(1)
+    forward(-1)
+    forward(1)
     kv_step(6)
-    y_step(0, 2)
+    each_y(1)
     kv_ready(2)
     forward(-2)
     forward(2)
-    for m in range(3):
-        y_step(1, m)
+    each_y(2)
     kv_ready(3)
     forward(-3)
     forward(3)
-    for m in range(3):
-        y_step(2, m)
     kv_ready(4)
     forward(4)
     normalize()
-    for m in range(3):
-        y_step(3, m)
+    each_y(3)
     backward(4)
+    backward(-3)
     grad_step(0)
-    backward(-3)
     activate()
     backward(3)
     grad_step(1)
+    backward(-2)
     gather_step(1)
+    backward(2)
+    grad_step(2)
+    backward(-1)
+    gather_step(2)
+    backward(1)
+    grad_step(3)
     gather_ready(0)
     experts_out(0)
-    backward(-2)
-    backward(2)
-    grad_step(2)
-    gather_step(2)
+    gather_step(3)
+    backward(0)
+    grad_step(4)
     gather_ready(1)
     experts_out(1)
-    backward(-1)
-    backward(1)
-    grad_step(3)
-    gather_step(3)
+    gather_step(4)
+    grad_step(5)
     gather_ready(2)
     experts_out(2)
-    backward(0)
-    grad_step(4)
-    gather_step(4)
     gather_ready(3)
     experts_out(3)
-    grad_step(5)
     gather_ready(4)
     experts_out(4)
+    grad_step(6)
     query_grad()
-    grad_step(6)
     spread()
     spread_end()
     ret_finish()
     ret_local.wait()
     for c in sends:
         c.wait_send()
-    for core in range(2):
-
-        @pl.when(k == core)
-        def _(core=core):
-            for make, args in core_sends[core]:
-                make(*args).wait_send()
+    drain(s_km, kv.at[k])
+    drain(s_y, ysend)
+    drain(s_g, full.at[k, pl.ds(0, 7)])
+    drain(s_gm, full.at[k])
+    drain(s_dm, dkv.at[1 - k])
+
+    def drain_zero(start):
+        drain(s_kx, kv.at[k, 0, pl.ds(0, 3)])
+        drain(s_kz, kv.at[k, pl.ds(0, 7)])
+        drain(s_z, zsend)
+        drain(s_x, xsend.at[pl.ds(0, 3)])
+
+    def drain_one(start):
+        drain(s_kx, kv.at[k, :, pl.ds(0, 3)])
+        drain(s_kz, kv.at[k, pl.ds(0, 7), 0])
+        drain(s_z, zsend.at[pl.ds(0, 7)])
+        drain(s_x, xsend)
+
+    by_core(drain_zero, drain_one)
 
 
 def vmem():
@@ -865,8 +870,8 @@
     def b16(*dims):
         return pltpu.VMEM(dims, BF16)
 
-    sems = [5, 4, NE, NE, 24, 24, 32, 32, 8, 8, 24, 24, 21, 21, 21, 21, 24, 24]
-    sems += [8, 8, 14, 14, 24, 24, 1, 1, 3, 3, 4, 4, NE, NE]
+    sems = [5, 4, 1, 1, 1, 24, 1, 32, 1, 8, 3, 3, 1, 21, 1, 21, 1, 8]
+    sems += [1, 8, 1, 14, 1, 24, 1, 1, 3, 3, 4, 4, 1, 1]
     attn_out, dq, returned, kvg = call(
         layer_kernel,
         (shape(*q.shape), shape(*q.shape), shape(NE, SLAB, 128), shape(2, TOK, 4 * HEAD)),

time: 101 us -> 92.2 us (0.913)
  Pallas kernels: 100 us -> 91.4 us
    pallas_call x2, Pallas kernels: 100 us -> 91.4 us  [call(): pl.pallas_call(kernel, out_shape=outs, in_specs=specs or [vmem()] * len(a...]
where the time goes in v4:
time: 92.2 us; the launch traced here: 92 us
  Pallas kernels  91.4 us (99%)
    pallas_call x2, Pallas kernels, call(): pl.pallas_call(kernel, out_shape=outs, in_specs=specs or [vmem()] * len(a...  91.4 us

profile of v4, /device:TPU:1, one launch (start us, length us, event | category | flops | bytes accessed | tf_op | source)
XLA Modules:
  0.0 92.0 jit_solution(10982127048507490136)
XLA Ops:
  0.6 88.2 %layer.1 = (bf16[128,512]{1,0:T(8,128)(2,1)}, bf16[128,512]{1,0:T(8,128)(2,1)}, bf16[32,48,128]{2,1,0:T(8,128)(2,1)}, bf16[2,128,512]{2,1,0:T(8,128)(2,1)}) custom-call(s32[2,128]{1,0:T(2,128)} %bitcast.4, f32[2,128]{1,0:T(2,128)} %bitcast.6, bf16[128,256]{1,0:T(8,128)(2,1)} %x_ref.1, bf16[128,256]{1,0:T(8,128)(2,1)} %g_ref.1, bf16[128,512]{1,0:T(8,128)(2,1)} %key_ref.1, ...), custom_call_target="tpu_custom_call" | custom-call | tf_op jit(solution)/shard_map/layer/pallas_call | solution.py:845
  88.8 3.2 %combine.1 = (bf16[128,256]{1,0:T(8,128)(2,1)}, bf16[128,256]{1,0:T(8,128)(2,1)}, bf16[128,512]{1,0:T(8,128)(2,1)}, bf16[128,512]{1,0:T(8,128)(2,1)}, bf16[128,5...) custom-call(s32[2,128]{1,0:T(2,128)} %bitcast.5, f32[2,128]{1,0:T(2,128)} %bitcast.7, bf16[1536,128]{1,0:T(8,128)(2,1)} %bitcast.3, ...), custom_call_target="tpu_custom_call" | custom-call | tf_op jit(solution)/shard_map/combine/pallas_call | solution.py:845

commit v5 on v4

--- a/solution.py
+++ b/solution.py
@@ -227,6 +227,7 @@
 ORDER = [4, -3, 3, -2, 2, -1, 1, 0]
 STEPS = [0, -1, 1, -2, 2, -3, 3, 4]
 LANES = [0, -1, 1, -2]
+PEERS = [2, 1, -1]
 DEEP = NZ // 2
 KEYS = NX * TOK
 
@@ -596,26 +597,19 @@
     def x_start(start, s):
         for step in around(s):
             d, i = dkv_in(step), STEPS.index(step) * 3
-            for slot, xs in ((0, 2), (2, -1)):
+            for slot, xs in enumerate(PEERS):
                 j = here.at_x(xs)
                 xsend[i + slot] = add16(dkv[k, d, j], dmate[d, j]).astype(BF16)
-            start(xslot, i, 1)
-            start(xslot, i + 2, -1)
-
-    def x_mid(start, s):
-        for step in around(s):
-            d, i = here.at_z(step), STEPS.index(step) * 3
-            j = here.at_x(1)
-            xslot(i, 1).wait_recv()
-            xsend[i + 1] = add16(dkv[k, d, j], dmate[d, j], xrecv[i]).astype(BF16)
-            start(xslot, i + 1, 1)
+                start(xslot, i + slot, xs)
 
     def x_end(s):
         for step in around(s):
             d, i = here.at_z(step), STEPS.index(step) * 3
-            xslot(i + 2, -1).wait_recv()
-            xslot(i + 1, 1).wait_recv()
-            sums[i // 3] = add16(dkv[k, d, x], dmate[d, x], xrecv[i + 1], xrecv[i + 2])
+            for slot, xs in enumerate(PEERS):
+                xslot(i + slot, xs).wait_recv()
+            sums[i // 3] = add16(
+                dkv[k, d, x], dmate[d, x], xrecv[i], xrecv[i + 1], xrecv[i + 2]
+            )
 
     def grad_step(t):
         def zero(start):
@@ -630,30 +624,23 @@
                         zslot(2 * i + h, 2, 1 if i == 3 else -1).wait_recv()
                 last = pl.ds(4 * (2 * DEEP - 2), 4)
                 sums[0:4] = add16(dkv[k, d], dmate[d], zrecv[12:16], zrecv[last])
-                xsend[0] = sums[here.at_x(2)].astype(BF16)
-                start(xslot, 0, 1)
-                xsend[2] = sums[here.at_x(-1)].astype(BF16)
-                start(xslot, 2, -1)
-            elif t == DEEP + 1:
-                xslot(0, 1).wait_recv()
-                xsend[1] = (sums[here.at_x(1)] + xrecv[0].astype(F32)).astype(BF16)
-                start(xslot, 1, 1)
+                for slot, xs in enumerate(PEERS):
+                    xsend[slot] = sums[here.at_x(xs)].astype(BF16)
+                    start(xslot, slot, xs)
             else:
-                xslot(2, -1).wait_recv()
-                xslot(1, 1).wait_recv()
-                tsend[...] = (sums[x] + add16(xrecv[2], xrecv[1])).astype(BF16)
+                for slot, xs in enumerate(PEERS):
+                    xslot(slot, xs).wait_recv()
+                tsend[...] = (sums[x] + add16(xrecv[0], xrecv[1], xrecv[2])).astype(BF16)
 
         def one(start):
             if t <= DEEP:
                 x_start(start, DEEP - t)
-            if 1 <= t <= DEEP + 1:
-                x_mid(start, DEEP + 1 - t)
-            if t >= 2:
-                x_end(DEEP + 2 - t)
-                if t < DEEP + 2:
-                    thin_step(start, t - 2, 1)
-                    if t > 2:
-                        thin_step(start, t - 3, -1)
+            if t >= 1:
+                x_end(DEEP + 1 - t)
+                if t <= DEEP:
+                    thin_step(start, t - 1, 1)
+                    if t > 1:
+                        thin_step(start, t - 2, -1)
                 else:
                     zslot(DEEP - 1, 1, 1).wait_recv()
                     zslot(2 * DEEP - 2, 1, -1).wait_recv()
@@ -661,7 +648,7 @@
                     tsend[...] = total.astype(BF16)
 
         by_core(zero, one)
-        if t == DEEP + 2:
+        if t == DEEP + 1:
             go(twin)
 
     twin = remote(tsend, trecv, s_t.at[0], r_t.at[0], here.twin)
@@ -742,6 +729,8 @@
         c.wait()
     stack()
     kv_step(2)
+    kv_ready(0)
+    forward(0)
     kv_step(3)
     local.wait()
     finish()
@@ -754,8 +743,6 @@
     y_step(0, 1)
     kv_step(5)
     y_step(0, 2)
-    kv_ready(0)
-    forward(0)
     kv_ready(1)
     forward(-1)
     forward(1)
@@ -786,24 +773,23 @@
     gather_step(2)
     backward(1)
     grad_step(3)
+    backward(0)
+    gather_step(3)
+    grad_step(4)
     gather_ready(0)
     experts_out(0)
-    gather_step(3)
-    backward(0)
-    grad_step(4)
+    gather_step(4)
     gather_ready(1)
     experts_out(1)
-    gather_step(4)
     grad_step(5)
     gather_ready(2)
     experts_out(2)
     gather_ready(3)
+    spread()
     experts_out(3)
     gather_ready(4)
     experts_out(4)
-    grad_step(6)
     query_grad()
-    spread()
     spread_end()
     ret_finish()
     ret_local.wait()

time: 92.2 us -> 88.8 us (0.963)
  Pallas kernels: 91.4 us -> 87.9 us
    pallas_call x2, Pallas kernels: 91.4 us -> 87.9 us  [call(): pl.pallas_call(kernel, out_shape=outs, in_specs=specs or [vmem()] * len(a...]
where the time goes in v5:
time: 88.8 us; the launch traced here: 88.6 us
  Pallas kernels  87.9 us (99%)
    pallas_call x2, Pallas kernels, call(): pl.pallas_call(kernel, out_shape=outs, in_specs=specs or [vmem()] * len(a...  87.9 us

profile of v5, /device:TPU:1, one launch (start us, length us, event | category | flops | bytes accessed | tf_op | source)
XLA Modules:
  0.0 88.6 jit_solution(14060823575799868596)
XLA Ops:
  0.6 84.7 %layer.1 = (bf16[128,512]{1,0:T(8,128)(2,1)}, bf16[128,512]{1,0:T(8,128)(2,1)}, bf16[32,48,128]{2,1,0:T(8,128)(2,1)}, bf16[2,128,512]{2,1,0:T(8,128)(2,1)}) custom-call(s32[2,128]{1,0:T(2,128)} %bitcast.4, f32[2,128]{1,0:T(2,128)} %bitcast.6, bf16[128,256]{1,0:T(8,128)(2,1)} %x_ref.1, bf16[128,256]{1,0:T(8,128)(2,1)} %g_ref.1, bf16[128,512]{1,0:T(8,128)(2,1)} %key_ref.1, ...), custom_call_target="tpu_custom_call" | custom-call | tf_op jit(solution)/shard_map/layer/pallas_call | solution.py:831
  85.3 3.2 %combine.1 = (bf16[128,256]{1,0:T(8,128)(2,1)}, bf16[128,256]{1,0:T(8,128)(2,1)}, bf16[128,512]{1,0:T(8,128)(2,1)}, bf16[128,512]{1,0:T(8,128)(2,1)}, bf16[128,5...) custom-call(s32[2,128]{1,0:T(2,128)} %bitcast.5, f32[2,128]{1,0:T(2,128)} %bitcast.7, bf16[1536,128]{1,0:T(8,128)(2,1)} %bitcast.3, ...), custom_call_target="tpu_custom_call" | custom-call | tf_op jit(solution)/shard_map/combine/pallas_call | solution.py:831

commit v6 on v5

--- a/solution.py
+++ b/solution.py
@@ -84,24 +84,25 @@
     hit0 = jnp.where(y0 == want, 1.0, 0.0)
     hit1 = jnp.where(y1 == want, 1.0, 0.0)
     both = hit0 + hit1
-    q = [jnp.where(quarter == float(i), 1.0, 0.0) for i in range(4)]
-    table = jnp.concatenate(
-        [both * q[0], both * q[1], hit0 * q[2], hit0 * q[3], hit1 * q[2], hit1 * q[3]], axis=1
-    ).astype(BF16)
     x = x_ref[...]
     g = g_ref[...].astype(F32)
     gain = gain_ref[...]
     w0, w1 = column(gain[0:1]), column(gain[1:2])
     lo, hi = g[:, :128], g[:, 128:]
-    scaled = [(a * w).astype(BF16) for w in (w0, w1) for a in (lo, hi)]
-    rows = jnp.concatenate([x[:, :128], x[:, 128:]] + scaled, axis=0)
-    out_ref[...] = dot(table, rows).astype(BF16).reshape(NE, SLAB, 128)
-
-
-def combine_kernel(
-    ids_ref, gain_ref, back_ref, kvg_ref, ao_ref, dq_ref,
-    out_ref, in_ref, kg_ref, vg_ref, ao_out, dq_out,
-):
+    s0 = jnp.concatenate([lo * w0, hi * w0], axis=1).astype(BF16)
+    s1 = jnp.concatenate([lo * w1, hi * w1], axis=1).astype(BF16)
+    rows = dot(both.astype(BF16), x)
+    hits = jnp.concatenate([hit0, hit1], axis=1).astype(BF16)
+    scaled = dot(hits, jnp.concatenate([s0, s1], axis=0))
+    out = jnp.where(
+        quarter < 2.0,
+        jnp.where(quarter < 1.0, rows[:, :128], rows[:, 128:]),
+        jnp.where(quarter < 3.0, scaled[:, :128], scaled[:, 128:]),
+    )
+    out_ref[...] = out.astype(BF16).reshape(NE, SLAB, 128)
+
+
+def combine_tables(ids_ref, tab_ref):
     v0, v1 = route_tables(ids_ref[...])
     total = NE * SLAB
     expert, quarter, slot = slab_index(fiota((1, total), 1))
@@ -111,18 +112,29 @@
     want = slot + 1.0
     hit0 = jnp.where(y0 == want, 1.0, 0.0)
     hit1 = jnp.where(y1 == want, 1.0, 0.0)
-    both = hit0 + hit1
     q = [jnp.where(quarter == float(i), 1.0, 0.0) for i in range(4)]
-    back = back_ref[...]
+    for i in range(2):
+        tab_ref[i] = (hit0 * q[i]).astype(BF16)
+        tab_ref[2 + i] = (hit1 * q[i]).astype(BF16)
+        tab_ref[4 + i] = ((hit0 + hit1) * q[2 + i]).astype(BF16)
+
+
+def combine(gain_ref, tab_ref, ret_ref, out_ref, in_ref):
+    back = ret_ref[...].reshape(NE * SLAB, 128)
     gain = gain_ref[...]
     w0, w1 = column(gain[0:1]), column(gain[1:2])
     for i in range(2):
-        part0 = dot((hit0 * q[i]).astype(BF16), back)
-        part1 = dot((hit1 * q[i]).astype(BF16), back)
-        out_ref[:, i * 128 : (i + 1) * 128] = (part0 * w0 + part1 * w1).astype(BF16)
-        in_ref[:, i * 128 : (i + 1) * 128] = dot((both * q[2 + i]).astype(BF16), back).astype(BF16)
+        lanes = slice(i * 128, (i + 1) * 128)
+        mixed = dot(tab_ref[i], back) * w0 + dot(tab_ref[2 + i], back) * w1
+        out_ref[:, lanes] = mixed.astype(BF16)
+        in_ref[:, lanes] = dot(tab_ref[4 + i], back).astype(BF16)
+
+
+def close_kernel(mo_ref, ig_ref, kvg_ref, ao_ref, dq_ref, mo_out, ig_out, kg_ref, vg_ref, ao_out, dq_out):
     kg_ref[...] = kvg_ref[0]
     vg_ref[...] = kvg_ref[1]
+    mo_out[...] = mo_ref[...]
+    ig_out[...] = ig_ref[...]
     ao_out[...] = ao_ref[...]
     dq_out[...] = dq_ref[...]
 
@@ -242,8 +254,8 @@
 
 def layer_kernel(
     ids_ref, gain_ref, x_ref, g_ref, key_ref, val_ref, q_hbm, do_hbm, gate_hbm, up_hbm, down_hbm,
-    ao_ref, dq_ref, ret_ref, kvg_ref,
-    q_ref, do_ref, gate_ref, up_ref, down_ref,
+    ao_ref, dq_ref, mo_ref, ig_ref, kvg_ref,
+    ret_ref, tab_ref, q_ref, do_ref, gate_ref, up_ref, down_ref,
     send, recv, rows_ref, part, pmate, ysend, yrecv, full,
     kv, qs, dos, e_ref, mj, m_ref, l_ref, o_ref, d_ref, dq_acc,
     dkv, dmate, zsend, zrecv, sums, xsend, xrecv, tsend, trecv, kg, back,
@@ -790,9 +802,11 @@
     gather_ready(4)
     experts_out(4)
     query_grad()
+    combine_tables(ids_ref, tab_ref)
     spread_end()
     ret_finish()
     ret_local.wait()
+    combine(gain_ref, tab_ref, ret_ref, mo_ref, ig_ref)
     for c in sends:
         c.wait_send()
     drain(s_km, kv.at[k])
@@ -858,10 +872,12 @@
 
     sems = [5, 4, 1, 1, 1, 24, 1, 32, 1, 8, 3, 3, 1, 21, 1, 21, 1, 8]
     sems += [1, 8, 1, 14, 1, 24, 1, 1, 3, 3, 4, 4, 1, 1]
-    attn_out, dq, returned, kvg = call(
+    attn_out, dq, moe_out, input_grad, kvg = call(
         layer_kernel,
-        (shape(*q.shape), shape(*q.shape), shape(NE, SLAB, 128), shape(2, TOK, 4 * HEAD)),
+        (shape(*q.shape), shape(*q.shape), shape(*x.shape), shape(*x.shape),
+         shape(2, TOK, 4 * HEAD)),
         [
+            b16(NE, SLAB, 128), b16(6, TOK, NE * SLAB),
             b16(*q.shape), b16(*do.shape), b16(*gate.shape), b16(*up.shape), b16(*down.shape),
             b16(NE, SLAB, 128), b16(NE, SLAB, 128), b16(2, ROWS, 256),
             b16(2, NY, 3, *yslab), b16(NY, 3, *yslab), b16(21, *yslab), b16(21, *yslab),
@@ -878,10 +894,10 @@
         specs=[vmem()] * 4 + [hbm] * 7, collective=0, name="layer",
     )
     moe_out, input_grad, key_grad, value_grad, attn_out, dq = call(
-        combine_kernel,
+        close_kernel,
         (shape(TOK, 256), shape(TOK, 256), shape(TOK, 512), shape(TOK, 512),
          shape(*q.shape), shape(*q.shape)), [],
-        ids, gain, returned.reshape(NE * SLAB, 128), kvg, attn_out, dq, name="combine",
+        moe_out, input_grad, kvg, attn_out, dq, name="close",
     )
     return attn_out, dq, key_grad, value_grad, moe_out, input_grad
 

time: 88.8 us -> 88.6 us (level)
  no operation moved by 1% of the time
where the time goes in v6:
time: 88.6 us; the launch traced here: 88.4 us
  Pallas kernels  87.7 us (99%)
    pallas_call x2, Pallas kernels, call(): pl.pallas_call(kernel, out_shape=outs, in_specs=specs or [vmem()] * len(a...  87.7 us

profile of v6, /device:TPU:1, one launch (start us, length us, event | category | flops | bytes accessed | tf_op | source)
XLA Modules:
  0.0 88.4 jit_solution(10469984974080295843)
XLA Ops:
  0.6 85.8 %layer.1 = (bf16[128,512]{1,0:T(8,128)(2,1)}, bf16[128,512]{1,0:T(8,128)(2,1)}, bf16[128,256]{1,0:T(8,128)(2,1)}, bf16[128,256]{1,0:T(8,128)(2,1)}, bf16[2,128,512]{2,1,0:T(8,128)(2,1)}) custom-call(s32[2,128]{1,0:T(2,128)} %bitcast.2, f32[2,128]{1,0:T(2,128)} %bitcast.3, bf16[128,256]{1,0:T(8,128)(2,1)} %x_ref.1, bf16[128,256]{1,0:T(8,128)(2,1)} %g_ref.1, ...), custom_call_target="tpu_custom_call" | custom-call | tf_op jit(solution)/shard_map/layer/pallas_call | solution.py:845
  86.4 2.0 %close.1 = (bf16[128,256]{1,0:T(8,128)(2,1)}, bf16[128,256]{1,0:T(8,128)(2,1)}, bf16[128,512]{1,0:T(8,128)(2,1)}, bf16[128,512]{1,0:T(8,128)(2,1)}, bf16[128,512]{1,0:T(8,128)(2,1)}, /*index=5*/bf16[128,512]{1,0:T(8,128)(2,1)}) custom-call(bf16[128,256]{1,0:T(8,128)(2,1)} %get-tuple-element.17.mo_ref, bf16[128,256]{1,0:T(8,128)(2,1)} %get-tuple-element.18.ig_ref, ...), custom_call_target="tpu_custom_call" | custom-call | tf_op jit(solution)/shard_map/close/pallas_call | solution.py:845
